TPU v7x, 32 devices: a whole 2x2x4 slice. The times are simulated.
32 devices in a mesh: tile: 16 (over z, y, x), chan: 2 (over core).
Axes of the slice: x: 2, y: 2, z: 4, core: 2. Of those that a mesh axis runs over, the one named last changes fastest.
Arguments:
- tile_features: bfloat16 [128, 128, 1024], P('tile', 'chan'), may hold values from -6 to 6
- conv_weight: bfloat16 [128, 128, 3, 3], P('chan'), may hold values from -0.1875 to 0.1875
- merge_weight: bfloat16 [128, 4, 256], replicated, may hold values from -0.25 to 0.25
- tissue: int32 [128], P('tile'), may hold values 0 or 1
- group_tiles: int32 [32, 4], P('tile'), may hold values from 0 to 127, as said below
- neighbours: int32 [32, 8], P('tile'), may hold values from -1 to 31, as said below
- merged_grad: bfloat16 [32, 256, 1024], P('tile', 'chan'), may hold values from -0.032958984 to 0.032958984
Outputs:
- merged: bfloat16 [32, 256, 1024], P('tile', 'chan')
- grad_conv: float32 [128, 128, 3, 3], replicated
- grad_merge: float32 [128, 4, 256], replicated
Inputs may be any that keep to these rules, and one draw needn't show every extreme that they name: `group_tiles`: row g lists the tiles of group g at top-left, top-right, bottom-left and bottom-right; every tile stands in exactly one row, and all four are held by the device that holds group g (tile t on index t // 8 of tile, group g on index g // 2). `neighbours`: entry e of row g names the group beside group g in direction e (0 up, 1 down, 2 left, 3 right, 4 up-left, 5 up-right, 6 down-left, 7 down-right) on the same slide, or -1 where there is none. The relation is mutual: entry e of g names h exactly when entry o(e) of h names g, o swapping 0 with 1, 2 with 3, 4 with 7, 5 with 6. With p = g // 2 and r = g % 2, a named group is h = q * 2 + r + u, where u = -1, 1, 0, 0, -1, -1, 1, 1 and v = 0, 0, -1, 1, -1, 1, -1, 1 for e = 0 .. 7 and q = (p + v + 4 * u) modulo the size of tile. The entries of one device's groups name groups of any single other device at most 2 times, and some device reaches that count.
All inputs are finite; a program needn't handle non-finite values. No bound on the sum of `tissue` on one device may be relied on, other than what follows from the above.
Results may differ from a plain program's by a relative error of at most 0.0049.
Values may be sent and summed in bfloat16 or wider, within the bound.
A program may use at most 64 MiB of HBM per device.

v0:
```python
import jax
import jax.numpy as jnp
from jax import lax
from jax.sharding import PartitionSpec as P

PIX = 32


OPPOSITE = (1, 0, 3, 2, 7, 6, 5, 4)
ROW_STEPS = (-1, 1, 0, 0, -1, -1, 1, 1)
COLUMN_STEPS = (0, 0, -1, 1, -1, 1, -1, 1)


def passed_along(block, axis, distance):
    devices = range(lax.axis_size(axis))
    route = [((i - distance) % len(devices), i) for i in devices]
    return lax.ppermute(block, axis, route)


def boundary(picture):
    top_row = picture[:, :, 0, :]
    bottom_row = picture[:, :, -1, :]
    left_column = picture[:, :, :, 0]
    right_column = picture[:, :, :, -1]
    return jnp.stack(
        [top_row, bottom_row, left_column, right_column, top_row, top_row, bottom_row, bottom_row],
        axis=1,
    )


def assemble(tile_rows, local_ids, width):
    number = local_ids.shape[0]
    channels = tile_rows.shape[1]
    picked = jnp.take(tile_rows, local_ids.reshape(-1), axis=0)
    picked = picked.reshape(number, 2, 2, channels, width, width)
    return picked.transpose(0, 3, 1, 4, 2, 5).reshape(number, channels, 2 * width, 2 * width)


def framed(picture, rim_cells):
    extent = picture.shape[2]
    upper = jnp.concatenate(
        [rim_cells[:, 4, :, extent - 1 :], rim_cells[:, 0], rim_cells[:, 5, :, :1]], axis=2
    )
    lower = jnp.concatenate(
        [rim_cells[:, 6, :, extent - 1 :], rim_cells[:, 1], rim_cells[:, 7, :, :1]], axis=2
    )
    middle = jnp.concatenate(
        [rim_cells[:, 2][..., None], picture, rim_cells[:, 3][..., None]], axis=3
    )
    return jnp.concatenate([upper[:, :, None, :], middle, lower[:, :, None, :]], axis=2)


def tissue_map(tissue_rows, width):
    number = tissue_rows.shape[0]
    layout = tissue_rows.reshape(number, 2, 1, 2, 1)
    return jnp.broadcast_to(layout, (number, 2, width, 2, width)).reshape(
        number, 2 * width, 2 * width
    )


def to_blocks(hidden, width):
    number, channels = (hidden.shape[0], hidden.shape[1])
    shaped = hidden.reshape(number, channels, width, 2, width, 2)
    return shaped.transpose(0, 3, 5, 1, 2, 4).reshape(number, 4, channels, width * width)


def from_blocks(blocks, width):
    number, channels = (blocks.shape[0], blocks.shape[2])
    shaped = blocks.reshape(number, 2, 2, channels, width, width)
    return shaped.transpose(0, 3, 4, 1, 5, 2).reshape(number, channels, 2 * width, 2 * width)


def shards(tile_features, conv_weight, merge_weight, tissue, group_tiles, neighbours, merged_grad):
    chan_index = lax.axis_index("chan")
    local_groups = neighbours.shape[0]
    local_tiles = tile_features.shape[0]
    own_chan = tile_features.shape[1]
    own_merged = merged_grad.shape[1]
    extent = 2 * PIX
    local_ids = group_tiles % local_tiles
    own_picture = assemble(tile_features, local_ids, PIX)
    own_edges = boundary(own_picture)
    sides = []
    for direction in range(8):
        row_step = ROW_STEPS[direction]
        device_step = COLUMN_STEPS[direction] + 4 * row_step
        sending = own_edges[:, OPPOSITE[direction]]
        arrived = passed_along(sending, "tile", -device_step)
        blank = jnp.zeros((1, own_chan, extent), jnp.bfloat16)
        if row_step == 1:
            aligned = jnp.concatenate([arrived[1:], blank], axis=0)
        elif row_step == -1:
            aligned = jnp.concatenate([blank, arrived[:-1]], axis=0)
        else:
            aligned = arrived
        present_rows = (neighbours[:, direction] >= 0)[:, None, None]
        sides.append(jnp.where(present_rows, aligned, jnp.zeros((), jnp.bfloat16)))
    rim_flat = jnp.stack(sides, axis=2).reshape(local_groups, own_chan, 8 * extent)
    all_tiles, all_rims = (
        lax.all_gather(tile_features, "chan", axis=1, tiled=True),
        lax.all_gather(rim_flat, "chan", axis=1, tiled=True),
    )
    channels_all = all_tiles.shape[1]
    rim_cells = all_rims.reshape(local_groups, channels_all, 8, extent).transpose(0, 2, 1, 3)
    padded = framed(assemble(all_tiles, local_ids, PIX), rim_cells)
    conv_out = lax.conv_general_dilated(
        padded,
        conv_weight,
        (1, 1),
        "VALID",
        dimension_numbers=("NCHW", "OIHW", "NCHW"),
        preferred_element_type=jnp.float32,
    )
    tissue_rows = (
        jnp.take(tissue, local_ids.reshape(-1)).reshape(local_groups, 4).astype(jnp.float32)
    )
    hidden = (jnp.maximum(conv_out, 0.0) * tissue_map(tissue_rows, PIX)[:, None]).astype(
        jnp.bfloat16
    )
    hidden_blocks = to_blocks(hidden, PIX)
    merge_rows = lax.dynamic_slice_in_dim(merge_weight, chan_index * own_chan, own_chan, 0)
    every_block = lax.all_gather(hidden_blocks, "chan", axis=2, tiled=True)
    merge_columns = lax.dynamic_slice_in_dim(merge_weight, chan_index * own_merged, own_merged, 2)
    merged = jnp.einsum(
        "ckm,gkcq->gmq", merge_columns, every_block, preferred_element_type=jnp.float32
    ).astype(jnp.bfloat16)
    upstream = lax.all_gather(merged_grad, "chan", axis=1, tiled=True)
    grad_hidden = from_blocks(
        jnp.einsum("ckm,gmq->gkcq", merge_rows, upstream, preferred_element_type=jnp.float32), PIX
    )
    grad_pre = jnp.where(hidden > 0, grad_hidden, 0.0).astype(jnp.bfloat16)
    merge_term = jnp.einsum(
        "gmq,gkcq->ckm", upstream, hidden_blocks, preferred_element_type=jnp.float32
    )
    conv_term = lax.conv_general_dilated(
        padded,
        grad_pre,
        (1, 1),
        "VALID",
        dimension_numbers=("CNHW", "IOHW", "NCHW"),
        preferred_element_type=jnp.float32,
    )
    conv_term = conv_term.transpose(1, 0, 2, 3)
    summed_conv, summed_merge = lax.psum((conv_term, merge_term), "tile")
    grad_conv, grad_merge = (
        lax.all_gather(summed_conv, "chan", axis=0, tiled=True),
        lax.all_gather(summed_merge, "chan", axis=0, tiled=True),
    )
    return (merged, grad_conv, grad_merge)


def solution(mesh):
    placed = (
        P("tile", "chan", None),
        P("chan", None, None, None),
        P(),
        P("tile"),
        P("tile", None),
        P("tile", None),
        P("tile", "chan", None),
    )
    return jax.shard_map(
        shards,
        mesh=mesh,
        in_specs=placed,
        out_specs=(P("tile", "chan", None), P(), P()),
        check_vma=False,
    )
```

profile of v0, /device:TPU:0, one launch (start us, length us, event | category | flops | bytes accessed | tf_op | source)
XLA Modules:
  0.0 228.2 jit_solution(11958574967176491079)
XLA Ops:
  8.8 1.8 gather_fusion
  12.7 3.1 %collective-permute-start = (bf16[2,64,64]{1,2,0:T(8,128)(2,1)S(1)}, bf16[2,64,64]{1,2,0:T(8,128)(2,1)S(1)}, u32[]{:S(2)}, u32[]{:S(2)}) collective-permute-start(bf16[2,64,64]{1,2,0:T(8,128)(2,1)S(1)} %get-tuple-element.30), channel_id=1, source_target_pairs={{24,0},{26,2},{28,4},{30,6},{0,8},{2,10},{4,12},{6,14},{8,16},{10,... | collective-permute-start | bytes 49160 | tf_op jit(solution)/shard_map/ppermute | solution.py:17
  15.7 2.5 %collective-permute-start.4 = (bf16[2,64,64]{1,2,0:T(8,128)(2,1)S(1)}, bf16[2,64,64]{1,2,0:T(8,128)(2,1)S(1)}, u32[]{:S(2)}, u32[]{:S(2)}) collective-permute-start(bf16[2,64,64]{1,2,0:T(8,128)(2,1)S(1)} %get-tuple-element.30), channel_id=1, source_target_pairs={{22,0},{24,2},{26,4},{28,6},{30,8},{0,10},{2,12},{4,14},{6,16},{8,... | collective-permute-start | bytes 49160 | tf_op jit(solution)/shard_map/ppermute | solution.py:17
  18.2 2.4 %collective-permute-start.5 = (bf16[2,64,64]{1,2,0:T(8,128)(2,1)S(1)}, bf16[2,64,64]{1,2,0:T(8,128)(2,1)S(1)}, u32[]{:S(2)}, u32[]{:S(2)}) collective-permute-start(bf16[2,64,64]{1,2,0:T(8,128)(2,1)S(1)} %get-tuple-element.30), channel_id=1, source_target_pairs={{26,0},{28,2},{30,4},{0,6},{2,8},{4,10},{6,12},{8,14},{10,16},{12,... | collective-permute-start | bytes 49160 | tf_op jit(solution)/shard_map/ppermute | solution.py:17
  20.7 1.3 collective-permute-start.1
  22.0 1.4 collective-permute-start.6
  25.2 1.2 collective-permute-start.7
  26.5 1.3 collective-permute-start.2
  27.8 6.2 %collective-permute-done.2 = bf16[2,64,64]{1,2,0:T(8,128)(2,1)S(1)} collective-permute-done((bf16[2,64,64]{1,2,0:T(8,128)(2,1)S(1)}, bf16[2,64,64]{1,2,0:T(8,128)(2,1)S(1)}, u32[]{:S(2)}, u32[]{:S(2)}) %collective-permute-start.2) | collective-permute-done | bytes 16416 | tf_op jit(solution)/shard_map/ppermute | solution.py:17
  34.2 3.7 %collective-permute-done.3 = bf16[2,64,64]{1,2,0:T(8,128)(2,1)S(1)} collective-permute-done((bf16[2,64,64]{1,2,0:T(8,128)(2,1)S(1)}, bf16[2,64,64]{1,2,0:T(8,128)(2,1)S(1)}, u32[]{:S(2)}, u32[]{:S(2)}) %collective-permute-start.3) | collective-permute-done | bytes 16416 | tf_op jit(solution)/shard_map/ppermute | solution.py:17
  38.8 2.2 all_gather.18
  41.3 1.7 convolution_bitcast_fusion
  43.0 1.8 copy.92
  44.8 3.7 %copy.93 = bf16[2,64,32,2,32,2]{1,3,2,5,4,0:T(2,128)(2,1)S(1)} copy(bf16[2,64,32,2,32,2]{1,4,2,5,3,0:T(8,128)(2,1)} %bitcast.139) | data formatting | bytes 2097152 | tf_op jit(solution)/shard_map/transpose | solution.py:70
  48.6 3.6 %gather_fusion.1 = bf16[8,128,1024]{2,1,0:T(8,128)(2,1)} fusion(bf16[8,128,1024]{2,1,0:T(8,128)(2,1)} %all-gather.4.cloned.1.call-done, s32[1024]{0:T(1024)S(1)} %pad_clamp_fusion), kind=kCustom, calls=%fused_computation.1 | custom fusion | bytes 4194336 | tf_op jit(solution)/shard_map/jit(_take)/gather | solution.py:34
  52.2 3.9 %copy.80 = bf16[8,128,1024]{1,2,0:T(8,128)(2,1)} copy(bf16[8,128,1024]{2,1,0:T(8,128)(2,1)} %gather_fusion.1) | data formatting | bytes 4194304 | tf_op jit(solution)/shard_map/jit(_take)/gather | solution.py:34
  56.1 1.9 select_bitcast_fusion
  57.9 3.2 %copy.81 = bf16[2,128,2,32,2,32]{1,0,5,4,3,2:T(2,128)(2,1)S(1)} copy(bf16[2,128,2,32,2,32]{1,5,3,4,2,0:T(8,128)(2,1)S(1)} %select_bitcast_fusion) | data formatting | bytes 4194304 | tf_op jit(solution)/shard_map/transpose | solution.py:36
  61.2 7.4 %fusion.31 = bf16[128,66,2,66]{0,2,3,1:T(2,128)(2,1)S(1)} fusion(bf16[2,128,1,66]{1,0,3,2:T(2,128)(2,1)S(1)} %get-tuple-element.40, bf16[2,128,64,1]{1,0,3,2:T(2,128)(2,1)S(1)} %get-tuple-element.37, bf16[2,128,64,64]{1,0,3,2:T(2,128)(2,1)S(1)} %bitcast.136, bf16[2,128,64,1]{1,0,3,2:T(2,128)(2,1)S(1)} %get-tuple-element.38, ...), kind=kLoop, calls=%fused_computation.79 | loop fusion | flops 4460544 | bytes 4460544 | tf_op jit(solution)/shard_map/concatenate | solution.py:50
  68.6 1.7 pad.6
  71.3 5.8 %select_maximum_fusion = f32[64,16,9,64]{3,1,2,0:T(8,128)S(1)} fusion(pred[16,9]{0,1:T(8,128)(4,1)S(1)} %copy-done.6, bf16[64,128,3,3]{1,0,3,2:T(8,128)(2,1)S(1)} %copy-done.5, bf16[128,66,2,7,2]{0,3,2,4,1:T(8,128)(2,1)S(1)} %slice.130, bf16[128,66,2,8,9]{0,3,2,4,1:T(8,128)(2,1)S(1)} %copy.85), kind=kOutput, calls=%fused_computation.5 | convolution fusion | flops 1369055232 | bytes 5413008 | tf_op jit(solution)/shard_map/conv_general_dilated | solution.py:106
  77.1 1.5 copy.86
  78.6 1.8 select_convert_fusion
  80.4 13.5 %fusion.10 = f32[64,128,3,3]{1,0,3,2:T(8,128)} fusion(bf16[2,64,64,64]{1,2,3,0:T(8,128)(2,1)S(1)} %get-tuple-element.25, bf16[2,128,1,66]{1,0,3,2:T(2,128)(2,1)S(1)} %get-tuple-element.40, bf16[2,128,64,1]{1,0,3,2:T(2,128)(2,1)S(1)} %get-tuple-element.37, bf16[2,128,64,64]{1,0,3,2:T(2,128)(2,1)S(1)} %bitcast.137, ...), kind=kOutput, calls=%fused_computation.19 | convolution fusion | flops 1219110912 | bytes 3573760 | tf_op jit(solution)/shard_map/transpose | solution.py:143
  94.0 1.4 copy.88
  95.3 1.4 convolution_bitcast_fusion.2
  96.9 1.6 copy.89
  98.6 107.2 %all-reduce.9.cloned.1.call-done = (f32[64,128,3,3]{1,0,3,2:T(8,128)}, f32[64,4,256]{2,0,1:T(8,128)}) async-done(((f32[64,128,3,3]{1,0,3,2:T(8,128)}, f32[64,4,256]{2,0,1:T(8,128)}), (f32[64,128,3,3]{1,0,3,2:T(8,128)}, f32[64,4,256]{2,0,1:T(8,128)})) %all-reduce.9.cloned.1.call-update) | async-done | bytes 557072 | tf_op jit(solution)/shard_map/psum | solution.py:144
  205.7 2.4 %all_gather.22 = f32[128,128,3,3]{1,0,3,2:T(8,128)S(1)} all-gather(f32[64,128,3,3]{1,0,3,2:T(8,128)} %get-tuple-element.23), channel_id=1, replica_groups=mesh['tile'=16,'chan'=2] {'chan'}, dimensions={0}, use_global_device_ids=true | all-gather | bytes 884736 | tf_op jit(solution)/shard_map/all_gather | solution.py:146
  208.2 2.4 %all_gather.23 = f32[128,4,256]{2,0,1:T(8,128)S(1)} all-gather(f32[64,4,256]{2,0,1:T(8,128)} %get-tuple-element.24), channel_id=1, replica_groups=mesh['tile'=16,'chan'=2] {'chan'}, dimensions={0}, use_global_device_ids=true | all-gather | bytes 786432 | tf_op jit(solution)/shard_map/all_gather | solution.py:147
  211.7 5.4 %all-gather.6.cloned.1.call-done = bf16[2,4,128,1024]{3,2,1,0:T(8,128)(2,1)} async-done(((bf16[2,4,64,1024]{3,2,1,0:T(8,128)(2,1)}), bf16[2,4,128,1024]{3,2,1,0:T(8,128)(2,1)}) %all-gather.6.cloned.1.call-update) | async-done | bytes 2097168 | tf_op jit(solution)/shard_map/all_gather | solution.py:122
  217.1 2.3 %fusion.16 = bf16[2,128,1024]{1,2,0:T(8,128)(2,1)S(1)} fusion(bf16[2,4,128,1024]{3,2,1,0:T(8,128)(2,1)} %all-gather.6.cloned.1.call-done, bf16[128,4,128]{2,1,0:T(4,128)(2,1)S(1)} %constant_dynamic-slice_fusion.1), kind=kOutput, calls=%fused_computation.25 | convolution fusion | flops 268697600 | bytes 2752512 | tf_op jit(solution)/shard_map/ckm,gkcq->gmq/dot_general | solution.py:124
  (79 shorter events, 10.7 us)
Async XLA Ops:
  7.2 17.2 %copy-start = (bf16[128,4,256]{2,1,0:T(4,128)(2,1)S(1)}, bf16[128,4,256]{2,1,0:T(4,128)(2,1)}, u32[]{:S(2)}) copy-start(bf16[128,4,256]{2,1,0:T(4,128)(2,1)} %param.9) | copy-start | bytes 786436
  7.2 34.2 %all-gather.8.cloned.1.call-start = ((), (), s32[]{:S(2)}) async-start(), calls=%async_computation.2 | async-start | bytes 1572864 | tf_op jit(solution)/shard_map/all_gather | solution.py:127
  7.9 40.7 %all-gather.4.cloned.1.call-start = ((), (), s32[]{:S(2)}) async-start(), calls=%async_computation | async-start | bytes 3145728 | tf_op jit(solution)/shard_map/all_gather | solution.py:100
  12.0 11.6 %copy-start.1 = (s32[8]{0:T(128)S(1)}, s32[8]{0:T(128)}, u32[]{:S(2)}) copy-start(s32[8]{0:T(128)} %param.10) | copy-start | bytes 100
  12.1 12.3 %copy-start.4 = (s32[2,4]{1,0:T(2,128)S(1)}, s32[2,4]{1,0:T(2,128)}, u32[]{:S(2)}) copy-start(s32[2,4]{1,0:T(2,128)} %param.11) | copy-start | bytes 100
  12.1 12.4 %copy-start.3 = (s32[2,8]{1,0:T(2,128)S(1)}, s32[2,8]{1,0:T(2,128)}, u32[]{:S(2)}) copy-start(s32[2,8]{1,0:T(2,128)} %param.12) | copy-start | bytes 196
  12.7 12.5 %collective-permute-start = (bf16[2,64,64]{1,2,0:T(8,128)(2,1)S(1)}, bf16[2,64,64]{1,2,0:T(8,128)(2,1)S(1)}, u32[]{:S(2)}, u32[]{:S(2)}) collective-permute-start(bf16[2,64,64]{1,2,0:T(8,128)(2,1)S(1)} %get-tuple-element.30), channel_id=1, source_target_pairs={{24,0},{26,2},{28,4},{30,6},{0,8},{2,10},{4,12},{6,14},{8,16},{10,... | collective-permute-start | bytes 49160 | tf_op jit(solution)/shard_map/ppermute | solution.py:17
  15.7 18.4 %collective-permute-start.4 = (bf16[2,64,64]{1,2,0:T(8,128)(2,1)S(1)}, bf16[2,64,64]{1,2,0:T(8,128)(2,1)S(1)}, u32[]{:S(2)}, u32[]{:S(2)}) collective-permute-start(bf16[2,64,64]{1,2,0:T(8,128)(2,1)S(1)} %get-tuple-element.30), channel_id=1, source_target_pairs={{22,0},{24,2},{26,4},{28,6},{30,8},{0,10},{2,12},{4,14},{6,16},{8,... | collective-permute-start | bytes 49160 | tf_op jit(solution)/shard_map/ppermute | solution.py:17
  18.2 15.9 %collective-permute-start.5 = (bf16[2,64,64]{1,2,0:T(8,128)(2,1)S(1)}, bf16[2,64,64]{1,2,0:T(8,128)(2,1)S(1)}, u32[]{:S(2)}, u32[]{:S(2)}) collective-permute-start(bf16[2,64,64]{1,2,0:T(8,128)(2,1)S(1)} %get-tuple-element.30), channel_id=1, source_target_pairs={{26,0},{28,2},{30,4},{0,6},{2,8},{4,10},{6,12},{8,14},{10,16},{12,... | collective-permute-start | bytes 49160 | tf_op jit(solution)/shard_map/ppermute | solution.py:17
  20.7 5.8 %collective-permute-start.1 = (bf16[2,64,64]{1,2,0:T(8,128)(2,1)S(1)}, bf16[2,64,64]{1,2,0:T(8,128)(2,1)S(1)}, u32[]{:S(2)}, u32[]{:S(2)}) collective-permute-start(bf16[2,64,64]{1,2,0:T(8,128)(2,1)S(1)} %get-tuple-element.29), channel_id=1, source_target_pairs={{8,0},{10,2},{12,4},{14,6},{16,8},{18,10},{20,12},{22,14},{24,16},... | collective-permute-start | bytes 49160 | tf_op jit(solution)/shard_map/ppermute | solution.py:17
  22.0 12.1 %collective-permute-start.6 = (bf16[2,64,64]{1,2,0:T(8,128)(2,1)S(1)}, bf16[2,64,64]{1,2,0:T(8,128)(2,1)S(1)}, u32[]{:S(2)}, u32[]{:S(2)}) collective-permute-start(bf16[2,64,64]{1,2,0:T(8,128)(2,1)S(1)} %get-tuple-element.29), channel_id=1, source_target_pairs={{6,0},{8,2},{10,4},{12,6},{14,8},{16,10},{18,12},{20,14},{22,16},{... | collective-permute-start | bytes 49160 | tf_op jit(solution)/shard_map/ppermute | solution.py:17
  23.4 182.3 %all-reduce.9.cloned.1.call-start = ((), (), s32[]{:S(2)}) async-start(), calls=%async_computation.3 | async-start | bytes 1114112 | tf_op jit(solution)/shard_map/psum | solution.py:144
  25.2 9.0 %collective-permute-start.7 = (bf16[2,64,64]{1,2,0:T(8,128)(2,1)S(1)}, bf16[2,64,64]{1,2,0:T(8,128)(2,1)S(1)}, u32[]{:S(2)}, u32[]{:S(2)}) collective-permute-start(bf16[2,64,64]{1,2,0:T(8,128)(2,1)S(1)} %get-tuple-element.29), channel_id=1, source_target_pairs={{10,0},{12,2},{14,4},{16,6},{18,8},{20,10},{22,12},{24,14},{26,16}... | collective-permute-start | bytes 49160 | tf_op jit(solution)/shard_map/ppermute | solution.py:17
  26.5 7.5 %collective-permute-start.2 = (bf16[2,64,64]{1,2,0:T(8,128)(2,1)S(1)}, bf16[2,64,64]{1,2,0:T(8,128)(2,1)S(1)}, u32[]{:S(2)}, u32[]{:S(2)}) collective-permute-start(bf16[2,64,64]{1,2,0:T(8,128)(2,1)S(1)} %bitcast.145), channel_id=1, source_target_pairs={{30,0},{0,2},{2,4},{4,6},{6,8},{8,10},{10,12},{12,14},{14,16},{16,... | collective-permute-start | bytes 49160 | tf_op jit(solution)/shard_map/ppermute | solution.py:17
  34.0 3.9 %collective-permute-start.3 = (bf16[2,64,64]{1,2,0:T(8,128)(2,1)S(1)}, bf16[2,64,64]{1,2,0:T(8,128)(2,1)S(1)}, u32[]{:S(2)}, u32[]{:S(2)}) collective-permute-start(bf16[2,64,64]{1,2,0:T(8,128)(2,1)S(1)} %bitcast.144), channel_id=1, source_target_pairs={{2,0},{4,2},{6,4},{8,6},{10,8},{12,10},{14,12},{16,14},{18,16},{20... | collective-permute-start | bytes 49160 | tf_op jit(solution)/shard_map/ppermute | solution.py:17
  70.4 0.9 copy-start.5
  70.4 0.9 copy-start.6
  94.0 1.4 copy-start.2
  96.8 120.3 %all-gather.6.cloned.1.call-start = ((), (), s32[]{:S(2)}) async-start(), calls=%async_computation.1 | async-start | bytes 3145728 | tf_op jit(solution)/shard_map/all_gather | solution.py:122
Sparse Core Ops, SparseCore 0:
  9.6 11.7 all-gather.7
  23.6 11.0 all-gather.3
  96.9 108.7 all-reduce.8
  207.2 9.8 all-gather.5
where the time goes:
time: 232 us; the launch traced here: 228 us
  waiting for transfers between devices  123 us (53%)
  local copies, waits for them, and re-layouts  32.1 us (14%)
  matrix products  24.8 us (11%)
  between operations  14.6 us (6%)
  starting transfers between devices  13.4 us (6%)
  other arithmetic  13.1 us (6%)
  blocking collectives  6.97 us (3%)
    psum x1, waiting for transfers between devices, shards(): summed_conv, summed_merge = lax.psum((conv_term, merge_term), 'tile')  107 us
    transpose x1, matrix products, shards(): conv_term = conv_term.transpose(1, 0, 2, 3)  13.5 us
    ppermute x8, starting transfers between devices, passed_along(): return lax.ppermute(block, axis, route)  13.2 us
    gather x4, local copies, waits for them, and re-layouts, assemble(): picked = jnp.take(tile_rows, local_ids.reshape(-1), axis=0)  10.4 us
    ppermute x8, waiting for transfers between devices, passed_along(): return lax.ppermute(block, axis, route)  9.93 us
    concatenate x1, other arithmetic, framed(): jnp.concatenate([upper[:, :, None, :], middle, lower[:, :, None, :]], axi...  7.44 us
    conv_general_dilated x1, matrix products, shards(): lax.conv_general_dilated(padded, conv_weight, (1, 1), 'VALID', dimension_...  5.81 us
    all_gather x1, waiting for transfers between devices, shards(): every_block = lax.all_gather(hidden_blocks, 'chan', axis=2, tiled=True)  5.39 us
  transfers between devices with their start and end apart: 12, of which 4 were waited for; matrix products, arithmetic and copies ran while one was open for 8% of the time, Pallas kernels for 0%

commit v1 on v0

--- a/solution.py
+++ b/solution.py
@@ -1,6 +1,8 @@
 import jax
 import jax.numpy as jnp
 from jax import lax
+from jax.experimental import pallas as pl
+from jax.experimental.pallas import tpu as pltpu
 from jax.sharding import PartitionSpec as P
 
 PIX = 32
@@ -68,6 +70,90 @@
     number, channels = (blocks.shape[0], blocks.shape[2])
     shaped = blocks.reshape(number, 2, 2, channels, width, width)
     return shaped.transpose(0, 3, 4, 1, 5, 2).reshape(number, channels, 2 * width, 2 * width)
+
+
+MESH = pl.DeviceIdType.MESH
+LANES = 128
+
+
+def total_kernel(n, nc, part_ref, out_ref, recv, send_a, recv_a, send_b, recv_b, send_c, recv_c):
+    me = lax.axis_index("tile")
+    core = lax.axis_index("chan")
+    barrier = pltpu.get_barrier_semaphore()
+    for d in range(1, n):
+        pl.semaphore_signal(
+            barrier, inc=1, device_id=(lax.rem(me + d, n), core), device_id_type=MESH
+        )
+    for d in range(1, nc):
+        pl.semaphore_signal(
+            barrier, inc=1, device_id=(me, lax.rem(core + d, nc)), device_id_type=MESH
+        )
+    pl.semaphore_wait(barrier, n - 1 + nc - 1)
+
+    scatter = []
+    for d in range(1, n):
+        peer = lax.rem(me + d, n)
+        copy = pltpu.make_async_remote_copy(
+            src_ref=part_ref.at[peer],
+            dst_ref=recv.at[d],
+            send_sem=send_a.at[d],
+            recv_sem=recv_a.at[d],
+            device_id=(peer, core),
+            device_id_type=MESH,
+        )
+        copy.start()
+        scatter.append(copy)
+    total = part_ref[me].astype(jnp.float32)
+    for d in range(1, n):
+        scatter[d - 1].wait_recv()
+        total += recv[d].astype(jnp.float32)
+    out_ref[core, me] = total.astype(out_ref.dtype)
+
+    spread = []
+    for d in range(1, n):
+        copy = pltpu.make_async_remote_copy(
+            src_ref=out_ref.at[core, me],
+            dst_ref=out_ref.at[core, me],
+            send_sem=send_b.at[d],
+            recv_sem=recv_b.at[d],
+            device_id=(lax.rem(me + d, n), core),
+            device_id_type=MESH,
+        )
+        copy.start()
+        spread.append(copy)
+    for copy in spread:
+        copy.wait_recv()
+    crossing = []
+    for d in range(1, nc):
+        copy = pltpu.make_async_remote_copy(
+            src_ref=out_ref.at[core],
+            dst_ref=out_ref.at[core],
+            send_sem=send_c.at[d],
+            recv_sem=recv_c.at[d],
+            device_id=(me, lax.rem(core + d, nc)),
+            device_id_type=MESH,
+        )
+        copy.start()
+        crossing.append(copy)
+    for copy in scatter + spread:
+        copy.wait_send()
+    for copy in crossing:
+        copy.wait()
+
+
+def totals(parts, n, nc):
+    rows = parts.shape[1]
+    return pl.pallas_call(
+        lambda *refs: total_kernel(n, nc, *refs),
+        name="weight_totals",
+        out_shape=jax.ShapeDtypeStruct((nc, n, rows, LANES), parts.dtype),
+        in_specs=[pl.BlockSpec(memory_space=pltpu.VMEM)],
+        out_specs=pl.BlockSpec(memory_space=pltpu.VMEM),
+        scratch_shapes=[pltpu.VMEM((n, rows, LANES), parts.dtype)]
+        + [pltpu.SemaphoreType.DMA((n,))] * 4
+        + [pltpu.SemaphoreType.DMA((nc,))] * 2,
+        compiler_params=pltpu.CompilerParams(collective_id=0, has_side_effects=True),
+    )(parts)
 
 
 def shards(tile_features, conv_weight, merge_weight, tissue, group_tiles, neighbours, merged_grad):
@@ -141,10 +227,25 @@
         preferred_element_type=jnp.float32,
     )
     conv_term = conv_term.transpose(1, 0, 2, 3)
-    summed_conv, summed_merge = lax.psum((conv_term, merge_term), "tile")
-    grad_conv, grad_merge = (
-        lax.all_gather(summed_conv, "chan", axis=0, tiled=True),
-        lax.all_gather(summed_merge, "chan", axis=0, tiled=True),
+    n = lax.axis_size("tile")
+    nc = lax.axis_size("chan")
+    conv_rows = conv_term.transpose(2, 3, 0, 1).reshape(-1, LANES)
+    merge_rows_part = merge_term.reshape(-1, LANES)
+    stacked = jnp.concatenate([conv_rows, merge_rows_part], axis=0).astype(jnp.bfloat16)
+    used = stacked.shape[0]
+    rows = -(-used // (16 * n)) * 16
+    parts = jnp.pad(stacked, ((0, rows * n - used), (0, 0))).reshape(n, rows, LANES)
+    summed = totals(parts, n, nc).reshape(nc, n * rows, LANES)
+    conv_count = conv_rows.shape[0]
+    grad_conv = (
+        summed[:, :conv_count]
+        .reshape(nc, 3, 3, own_chan, channels_all)
+        .transpose(0, 3, 4, 1, 2)
+        .reshape(channels_all, channels_all, 3, 3)
+        .astype(jnp.float32)
+    )
+    grad_merge = (
+        summed[:, conv_count:used].reshape(merge_weight.shape).astype(jnp.float32)
     )
     return (merged, grad_conv, grad_merge)
 

time: 232 us -> 139 us (0.60)
  waiting for transfers between devices: 123 us -> 10.8 us
  Pallas kernels: 0 us -> 22.3 us
  matrix products: 24.8 us -> 32.5 us
  blocking collectives: 6.97 us -> 2.17 us
    psum x1 -> x0, waiting for transfers between devices: 107 us -> none  [shards(): summed_conv, summed_merge = lax.psum((conv_term, merge_term), 'tile')]
    pallas_call x0 -> x1, Pallas kernels: none -> 22.3 us  [totals(): pl.pallas_call(lambda *refs: total_kernel(n, nc, *refs), name='weight_tot...]
    another operation x0 -> x1, matrix products: none -> 15.8 us  [shards(): conv_rows = conv_term.transpose(2, 3, 0, 1).reshape(-1, LANES)]
    transpose x1 -> x0, matrix products: 13.5 us -> none  [shards(): conv_term = conv_term.transpose(1, 0, 2, 3)]
    conv_general_dilated x1, matrix products: 5.81 us -> 11.9 us  [shards(): lax.conv_general_dilated(padded, conv_weight, (1, 1), 'VALID', dimension_...]
    all_gather x1, waiting for transfers between devices: 5.39 us -> 0.01 us  [shards(): every_block = lax.all_gather(hidden_blocks, 'chan', axis=2, tiled=True)]
    all_gather x2 -> x0, blocking collectives: 4.81 us -> none  [the longest x1 2.43 us: shards(): lax.all_gather(summed_conv, 'chan', axis=0, tiled=True)]
  transfers between devices with their start and end apart: 12 -> 11, of which waited for: 4 -> 2; matrix products, arithmetic and copies ran while one was open for 8% -> 51% of each run, Pallas kernels for 0% -> 16%
where the time goes in v1:
time: 139 us; the launch traced here: 137 us
  matrix products  32.5 us (23%)
  local copies, waits for them, and re-layouts  31 us (22%)
  Pallas kernels  22.3 us (16%)
  between operations  14.1 us (10%)
  starting transfers between devices  13.3 us (10%)
  other arithmetic  11.3 us (8%)
  waiting for transfers between devices  10.8 us (8%)
  blocking collectives  2.17 us (2%)
    pallas_call x1, Pallas kernels, totals(): pl.pallas_call(lambda *refs: total_kernel(n, nc, *refs), name='weight_tot...  22.3 us
    another operation x1, matrix products, shards(): conv_rows = conv_term.transpose(2, 3, 0, 1).reshape(-1, LANES)  15.8 us
    ppermute x8, starting transfers between devices, passed_along(): return lax.ppermute(block, axis, route)  13.2 us
    conv_general_dilated x1, matrix products, shards(): lax.conv_general_dilated(padded, conv_weight, (1, 1), 'VALID', dimension_...  11.9 us
    ppermute x8, waiting for transfers between devices, passed_along(): return lax.ppermute(block, axis, route)  10 us
    gather x4, local copies, waits for them, and re-layouts, assemble(): picked = jnp.take(tile_rows, local_ids.reshape(-1), axis=0)  9.51 us
    concatenate x1, other arithmetic, framed(): jnp.concatenate([upper[:, :, None, :], middle, lower[:, :, None, :]], axi...  7.25 us
    transpose x1, local copies, waits for them, and re-layouts, from_blocks(): shaped.transpose(0, 3, 4, 1, 5, 2)  5.19 us
  transfers between devices with their start and end apart: 11, of which 2 were waited for; matrix products, arithmetic and copies ran while one was open for 51% of the time, Pallas kernels for 16%

profile of v1, /device:TPU:0, one launch (start us, length us, event | category | flops | bytes accessed | tf_op | source)
XLA Modules:
  0.0 137.4 jit_solution(14926663873041022371)
XLA Ops:
  8.8 1.8 %gather_fusion = bf16[8,64,1024]{2,1,0:T(8,128)(2,1)S(1)} fusion(bf16[8,64,1024]{2,1,0:T(8,128)(2,1)} %param.7, s32[1024]{0:T(1024)S(1)} %pad_clamp_fusion), kind=kCustom, calls=%fused_computation | custom fusion | bytes 2097184 | tf_op jit(solution)/shard_map/jit(_take)/gather | solution.py:36
  10.7 1.1 copy.63
  12.7 3.1 %collective-permute-start = (bf16[2,64,64]{1,2,0:T(8,128)(2,1)S(1)}, bf16[2,64,64]{1,2,0:T(8,128)(2,1)S(1)}, u32[]{:S(2)}, u32[]{:S(2)}) collective-permute-start(bf16[2,64,64]{1,2,0:T(8,128)(2,1)S(1)} %get-tuple-element.26), channel_id=1, source_target_pairs={{24,0},{26,2},{28,4},{30,6},{0,8},{2,10},{4,12},{6,14},{8,16},{10,... | collective-permute-start | bytes 49160 | tf_op jit(solution)/shard_map/ppermute | solution.py:19
  15.7 2.5 %collective-permute-start.4 = (bf16[2,64,64]{1,2,0:T(8,128)(2,1)S(1)}, bf16[2,64,64]{1,2,0:T(8,128)(2,1)S(1)}, u32[]{:S(2)}, u32[]{:S(2)}) collective-permute-start(bf16[2,64,64]{1,2,0:T(8,128)(2,1)S(1)} %get-tuple-element.26), channel_id=1, source_target_pairs={{22,0},{24,2},{26,4},{28,6},{30,8},{0,10},{2,12},{4,14},{6,16},{8,... | collective-permute-start | bytes 49160 | tf_op jit(solution)/shard_map/ppermute | solution.py:19
  18.2 2.4 %collective-permute-start.5 = (bf16[2,64,64]{1,2,0:T(8,128)(2,1)S(1)}, bf16[2,64,64]{1,2,0:T(8,128)(2,1)S(1)}, u32[]{:S(2)}, u32[]{:S(2)}) collective-permute-start(bf16[2,64,64]{1,2,0:T(8,128)(2,1)S(1)} %get-tuple-element.26), channel_id=1, source_target_pairs={{26,0},{28,2},{30,4},{0,6},{2,8},{4,10},{6,12},{8,14},{10,16},{12,... | collective-permute-start | bytes 49160 | tf_op jit(solution)/shard_map/ppermute | solution.py:19
  20.7 1.3 collective-permute-start.1
  22.0 1.4 %collective-permute-start.6 = (bf16[2,64,64]{1,2,0:T(8,128)(2,1)S(1)}, bf16[2,64,64]{1,2,0:T(8,128)(2,1)S(1)}, u32[]{:S(2)}, u32[]{:S(2)}) collective-permute-start(bf16[2,64,64]{1,2,0:T(8,128)(2,1)S(1)} %get-tuple-element.25), channel_id=1, source_target_pairs={{6,0},{8,2},{10,4},{12,6},{14,8},{16,10},{18,12},{20,14},{22,16},{... | collective-permute-start | bytes 49160 | tf_op jit(solution)/shard_map/ppermute | solution.py:19
  25.6 1.2 collective-permute-start.7
  26.8 1.2 collective-permute-start.2
  28.2 6.2 %collective-permute-done.2 = bf16[2,64,64]{1,2,0:T(8,128)(2,1)S(1)} collective-permute-done((bf16[2,64,64]{1,2,0:T(8,128)(2,1)S(1)}, bf16[2,64,64]{1,2,0:T(8,128)(2,1)S(1)}, u32[]{:S(2)}, u32[]{:S(2)}) %collective-permute-start.2) | collective-permute-done | bytes 16416 | tf_op jit(solution)/shard_map/ppermute | solution.py:19
  34.5 3.8 %collective-permute-done.3 = bf16[2,64,64]{1,2,0:T(8,128)(2,1)S(1)} collective-permute-done((bf16[2,64,64]{1,2,0:T(8,128)(2,1)S(1)}, bf16[2,64,64]{1,2,0:T(8,128)(2,1)S(1)}, u32[]{:S(2)}, u32[]{:S(2)}) %collective-permute-start.3) | collective-permute-done | bytes 16416 | tf_op jit(solution)/shard_map/ppermute | solution.py:19
  39.1 2.2 %all_gather.12 = bf16[2,128,512]{2,1,0:T(8,128)(2,1)S(1)} all-gather(bf16[2,64,512]{2,1,0:T(8,128)(2,1)S(1)} %reshape.165), channel_id=1, replica_groups=mesh['tile'=16,'chan'=2] {'chan'}, dimensions={1}, use_global_device_ids=true | all-gather | bytes 393216 | tf_op jit(solution)/shard_map/all_gather | solution.py:187
  41.7 3.6 %gather_fusion.1 = bf16[8,128,1024]{2,1,0:T(8,128)(2,1)} fusion(bf16[8,128,1024]{2,1,0:T(8,128)(2,1)} %all-gather.4.cloned.1.call-done, s32[1024]{0:T(1024)S(1)} %pad_clamp_fusion), kind=kCustom, calls=%fused_computation.1 | custom fusion | bytes 4194336 | tf_op jit(solution)/shard_map/jit(_take)/gather | solution.py:36
  45.3 3.0 %copy.72 = bf16[8,128,1024]{1,2,0:T(8,128)(2,1)S(1)} copy(bf16[8,128,1024]{2,1,0:T(8,128)(2,1)} %gather_fusion.1) | data formatting | bytes 4194304 | tf_op jit(solution)/shard_map/jit(_take)/gather | solution.py:36
  48.6 3.2 %copy.73 = bf16[2,128,2,32,2,32]{1,0,5,4,3,2:T(2,128)(2,1)S(1)} copy(bf16[2,128,2,32,2,32]{1,5,3,4,2,0:T(8,128)(2,1)S(1)} %select_bitcast_fusion) | data formatting | bytes 4194304 | tf_op jit(solution)/shard_map/transpose | solution.py:38
  51.9 7.2 %pad_maximum_fusion = bf16[2,128,66,66]{1,0,3,2:T(2,128)(2,1)S(1)} fusion(bf16[2,128,1,66]{1,0,3,2:T(2,128)(2,1)S(1)} %get-tuple-element.36, bf16[2,128,64,1]{1,0,3,2:T(2,128)(2,1)S(1)} %get-tuple-element.33, bf16[2,128,64,64]{1,0,3,2:T(2,128)(2,1)S(1)} %bitcast.129, bf16[2,128,64,1]{1,0,3,2:T(2,128)(2,1)S(1)} %get-tuple-element.34, ...), kind=kLoop, calls=%fused_computation.8 | loop fusion | flops 4460544 | bytes 4460544 | tf_op jit(solution)/shard_map/concatenate | solution.py:52
  59.4 0.8 copy-done.8
  60.2 11.9 %fusion.2 = bf16[2,64,64,64]{1,0,3,2:T(2,128)(2,1)S(1)} fusion(bf16[2,128,66,66]{1,0,3,2:T(2,128)(2,1)S(1)} %pad_maximum_fusion, bf16[64,128,3,3]{1,0,3,2:T(8,128)(2,1)S(1)} %copy-done.8, f32[2,64,64]{0,2,1:T(8,128)S(1)} %bitcast.136), kind=kOutput, calls=%fused_computation.7 | convolution fusion | flops 1209532416 | bytes 3459072 | tf_op jit(solution)/shard_map/conv_general_dilated | solution.py:192
  72.5 1.0 copy-done.4
  73.5 1.6 %copy.78 = bf16[2,4,64,1024]{3,2,1,0:T(8,128)(2,1)} copy(bf16[2,4,64,1024]{2,3,1,0:T(8,128)(2,1)S(1)} %bitcast.126) | data formatting | bytes 2097152 | tf_op jit(solution)/shard_map/reshape | solution.py:66
  75.1 1.7 %convolution_bitcast_fusion = bf16[2,4,64,1024]{3,2,0,1:T(8,128)(2,1)S(1)} fusion(bf16[2,256,1024]{2,1,0:T(8,128)(2,1)} %all-gather.8.cloned.1.call-done, bf16[64,4,256]{2,1,0:T(4,128)(2,1)S(1)} %constant_dynamic-slice_fusion), kind=kOutput, calls=%fused_computation.12 | convolution fusion | flops 268435456 | bytes 2228224 | tf_op jit(solution)/shard_map/ckm,gmq->gkcq/dot_general | solution.py:215
  76.8 1.8 %copy.81 = bf16[2,4,64,1024]{2,3,1,0:T(8,128)(2,1)} copy(bf16[2,4,64,1024]{3,2,0,1:T(8,128)(2,1)S(1)} %convolution_bitcast_fusion) | data formatting | bytes 2097152 | tf_op jit(solution)/shard_map/ckm,gmq->gkcq/transpose | solution.py:215
  78.6 5.2 %copy.82 = bf16[2,64,32,2,32,2]{1,0,5,4,3,2:T(2,128)(2,1)} copy(bf16[2,64,32,2,32,2]{1,4,2,5,3,0:T(8,128)(2,1)} %bitcast.131) | data formatting | bytes 2097152 | tf_op jit(solution)/shard_map/transpose | solution.py:72
  83.8 0.8 fusion.11
  84.8 15.8 %fusion.7 = bf16[3,3,64,128]{3,2,1,0:T(8,128)(2,1)S(1)} fusion(bf16[2,128,66,66]{1,0,3,2:T(2,128)(2,1)} %copy-done.3, bf16[2,64,64,64]{1,0,3,2:T(2,128)(2,1)} %bitcast.138, bf16[2,64,64,64]{1,0,3,2:T(2,128)(2,1)} %copy-done.4), kind=kOutput, calls=%fused_computation.17 | convolution fusion | flops 1210130432 | bytes 4474880 | tf_op jit(solution)/shard_map/transpose;transpose | solution.py:232
  101.3 22.3 %weight_totals.1 = bf16[2,16,80,128]{3,2,1,0:T(8,128)(2,1)} custom-call(bf16[16,80,128]{2,1,0:T(8,128)(2,1)} %bitcast.139), custom_call_target="tpu_custom_call" | custom-call | tf_op jit(solution)/shard_map/weight_totals/pallas_call | solution.py:146
  123.6 1.0 slice.136
  124.6 0.9 copy.85
  125.5 1.0 slice_convert_fusion
  126.5 1.0 reshape.177
  127.5 2.4 %fusion.6 = bf16[2,128,1024]{1,2,0:T(8,128)(2,1)S(1)} fusion(bf16[2,4,128,1024]{3,2,1,0:T(8,128)(2,1)} %all-gather.6.cloned.1.call-done, bf16[128,4,128]{2,1,0:T(4,128)(2,1)S(1)} %copy-done.5), kind=kOutput, calls=%fused_computation.15 | convolution fusion | flops 268697600 | bytes 2752512 | tf_op jit(solution)/shard_map/ckm,gkcq->gmq/dot_general | solution.py:210
  129.9 1.0 copy.86
  (77 shorter events, 7.9 us)
Async XLA Ops:
  7.2 17.2 %copy-start = (bf16[128,4,256]{2,1,0:T(4,128)(2,1)S(1)}, bf16[128,4,256]{2,1,0:T(4,128)(2,1)}, u32[]{:S(2)}) copy-start(bf16[128,4,256]{2,1,0:T(4,128)(2,1)} %param.9) | copy-start | bytes 786436
  7.2 34.5 %all-gather.4.cloned.1.call-start = ((), (), s32[]{:S(2)}) async-start(), calls=%async_computation | async-start | bytes 3145728 | tf_op jit(solution)/shard_map/all_gather | solution.py:186
  7.9 67.2 %all-gather.8.cloned.1.call-start = ((), (), s32[]{:S(2)}) async-start(), calls=%async_computation.2 | async-start | bytes 1572864 | tf_op jit(solution)/shard_map/all_gather | solution.py:213
  12.0 11.6 %copy-start.1 = (s32[8]{0:T(128)S(1)}, s32[8]{0:T(128)}, u32[]{:S(2)}) copy-start(s32[8]{0:T(128)} %param.10) | copy-start | bytes 100
  12.1 12.3 %copy-start.7 = (s32[2,4]{1,0:T(2,128)S(1)}, s32[2,4]{1,0:T(2,128)}, u32[]{:S(2)}) copy-start(s32[2,4]{1,0:T(2,128)} %param.11) | copy-start | bytes 100
  12.1 13.1 %copy-start.6 = (s32[2,8]{1,0:T(2,128)S(1)}, s32[2,8]{1,0:T(2,128)}, u32[]{:S(2)}) copy-start(s32[2,8]{1,0:T(2,128)} %param.12) | copy-start | bytes 196
  12.7 12.9 %collective-permute-start = (bf16[2,64,64]{1,2,0:T(8,128)(2,1)S(1)}, bf16[2,64,64]{1,2,0:T(8,128)(2,1)S(1)}, u32[]{:S(2)}, u32[]{:S(2)}) collective-permute-start(bf16[2,64,64]{1,2,0:T(8,128)(2,1)S(1)} %get-tuple-element.26), channel_id=1, source_target_pairs={{24,0},{26,2},{28,4},{30,6},{0,8},{2,10},{4,12},{6,14},{8,16},{10,... | collective-permute-start | bytes 49160 | tf_op jit(solution)/shard_map/ppermute | solution.py:19
  15.7 18.7 %collective-permute-start.4 = (bf16[2,64,64]{1,2,0:T(8,128)(2,1)S(1)}, bf16[2,64,64]{1,2,0:T(8,128)(2,1)S(1)}, u32[]{:S(2)}, u32[]{:S(2)}) collective-permute-start(bf16[2,64,64]{1,2,0:T(8,128)(2,1)S(1)} %get-tuple-element.26), channel_id=1, source_target_pairs={{22,0},{24,2},{26,4},{28,6},{30,8},{0,10},{2,12},{4,14},{6,16},{8,... | collective-permute-start | bytes 49160 | tf_op jit(solution)/shard_map/ppermute | solution.py:19
  18.2 20.2 %collective-permute-start.5 = (bf16[2,64,64]{1,2,0:T(8,128)(2,1)S(1)}, bf16[2,64,64]{1,2,0:T(8,128)(2,1)S(1)}, u32[]{:S(2)}, u32[]{:S(2)}) collective-permute-start(bf16[2,64,64]{1,2,0:T(8,128)(2,1)S(1)} %get-tuple-element.26), channel_id=1, source_target_pairs={{26,0},{28,2},{30,4},{0,6},{2,8},{4,10},{6,12},{8,14},{10,16},{12,... | collective-permute-start | bytes 49160 | tf_op jit(solution)/shard_map/ppermute | solution.py:19
  20.7 6.1 %collective-permute-start.1 = (bf16[2,64,64]{1,2,0:T(8,128)(2,1)S(1)}, bf16[2,64,64]{1,2,0:T(8,128)(2,1)S(1)}, u32[]{:S(2)}, u32[]{:S(2)}) collective-permute-start(bf16[2,64,64]{1,2,0:T(8,128)(2,1)S(1)} %get-tuple-element.25), channel_id=1, source_target_pairs={{8,0},{10,2},{12,4},{14,6},{16,8},{18,10},{20,12},{22,14},{24,16},... | collective-permute-start | bytes 49160 | tf_op jit(solution)/shard_map/ppermute | solution.py:19
  22.0 16.5 %collective-permute-start.6 = (bf16[2,64,64]{1,2,0:T(8,128)(2,1)S(1)}, bf16[2,64,64]{1,2,0:T(8,128)(2,1)S(1)}, u32[]{:S(2)}, u32[]{:S(2)}) collective-permute-start(bf16[2,64,64]{1,2,0:T(8,128)(2,1)S(1)} %get-tuple-element.25), channel_id=1, source_target_pairs={{6,0},{8,2},{10,4},{12,6},{14,8},{16,10},{18,12},{20,14},{22,16},{... | collective-permute-start | bytes 49160 | tf_op jit(solution)/shard_map/ppermute | solution.py:19
  23.4 104.1 %all-gather.6.cloned.1.call-start = ((), (), s32[]{:S(2)}) async-start(), calls=%async_computation.1 | async-start | bytes 3145728 | tf_op jit(solution)/shard_map/all_gather | solution.py:208
  25.6 13.0 %collective-permute-start.7 = (bf16[2,64,64]{1,2,0:T(8,128)(2,1)S(1)}, bf16[2,64,64]{1,2,0:T(8,128)(2,1)S(1)}, u32[]{:S(2)}, u32[]{:S(2)}) collective-permute-start(bf16[2,64,64]{1,2,0:T(8,128)(2,1)S(1)} %get-tuple-element.25), channel_id=1, source_target_pairs={{10,0},{12,2},{14,4},{16,6},{18,8},{20,10},{22,12},{24,14},{26,16}... | collective-permute-start | bytes 49160 | tf_op jit(solution)/shard_map/ppermute | solution.py:19
  26.8 7.5 %collective-permute-start.2 = (bf16[2,64,64]{1,2,0:T(8,128)(2,1)S(1)}, bf16[2,64,64]{1,2,0:T(8,128)(2,1)S(1)}, u32[]{:S(2)}, u32[]{:S(2)}) collective-permute-start(bf16[2,64,64]{1,2,0:T(8,128)(2,1)S(1)} %bitcast.146), channel_id=1, source_target_pairs={{30,0},{0,2},{2,4},{4,6},{6,8},{8,10},{10,12},{12,14},{14,16},{16,... | collective-permute-start | bytes 49160 | tf_op jit(solution)/shard_map/ppermute | solution.py:19
  34.3 3.9 %collective-permute-start.3 = (bf16[2,64,64]{1,2,0:T(8,128)(2,1)S(1)}, bf16[2,64,64]{1,2,0:T(8,128)(2,1)S(1)}, u32[]{:S(2)}, u32[]{:S(2)}) collective-permute-start(bf16[2,64,64]{1,2,0:T(8,128)(2,1)S(1)} %bitcast.145), channel_id=1, source_target_pairs={{2,0},{4,2},{6,4},{8,6},{10,8},{12,10},{14,12},{16,14},{18,16},{20... | collective-permute-start | bytes 49160 | tf_op jit(solution)/shard_map/ppermute | solution.py:19
  59.1 13.0 %copy-start.3 = (bf16[2,128,66,66]{1,0,3,2:T(2,128)(2,1)}, bf16[2,128,66,66]{1,0,3,2:T(2,128)(2,1)S(1)}, u32[]{:S(2)}) copy-start(bf16[2,128,66,66]{1,0,3,2:T(2,128)(2,1)S(1)} %pad_maximum_fusion) | copy-start | bytes 6690820
  59.1 1.1 copy-start.8
  72.1 1.4 copy-start.4
  78.6 5.2 %copy-start.2 = (bf16[2,256,1024]{2,1,0:T(8,128)(2,1)S(1)}, bf16[2,256,1024]{2,1,0:T(8,128)(2,1)}, u32[]{:S(2)}) copy-start(bf16[2,256,1024]{2,1,0:T(8,128)(2,1)} %all-gather.8.cloned.1.call-done) | copy-start | bytes 3145732
  101.3 26.2 %copy-start.5 = (bf16[128,4,128]{2,1,0:T(4,128)(2,1)S(1)}, bf16[128,4,128]{2,1,0:T(4,128)(2,1)}, u32[]{:S(2)}) copy-start(bf16[128,4,128]{2,1,0:T(4,128)(2,1)} %constant_dynamic-slice_fusion.1) | copy-start | bytes 393220
Sparse Core Ops, SparseCore 0:
  9.6 13.2 all-gather.3
  24.4 10.1 all-gather.7
  75.2 9.9 all-gather.5

commit v2 on v1

--- a/solution.py
+++ b/solution.py
@@ -1,4 +1,6 @@
 import jax
+import ml_dtypes
+import numpy as np
 import jax.numpy as jnp
 from jax import lax
 from jax.experimental import pallas as pl
@@ -250,6 +252,416 @@
     return (merged, grad_conv, grad_merge)
 
 
+def edge_picker():
+    picks = np.zeros((PIX * PIX, 4 * PIX), np.float32)
+    for i in range(PIX):
+        picks[i, i] = 1
+        picks[(PIX - 1) * PIX + i, PIX + i] = 1
+        picks[i * PIX, 2 * PIX + i] = 1
+        picks[i * PIX + PIX - 1, 3 * PIX + i] = 1
+    return picks.astype(ml_dtypes.bfloat16)
+
+
+def phase_picker():
+    picks = np.zeros((2, 8, PIX, 2, 2, 4, PIX), np.float32)
+    for side in range(2):
+        for row in range(8):
+            for x in range(PIX):
+                picks[side, row, x, row % 2, x % 2, row // 2, 16 * side + x // 2] = 1
+    return picks.reshape(512, 512).astype(ml_dtypes.bfloat16)
+
+
+def column_picker():
+    picks = np.zeros((2, 4 * PIX, 2, 16, PIX), np.float32)
+    for r in range(2):
+        for y in range(16):
+            picks[0, 3 * PIX + 2 * y + r, r, y, 0] = 1
+            picks[1, 2 * PIX + 2 * y + r, r, y, PIX - 1] = 1
+    return picks.reshape(256, 1024).astype(ml_dtypes.bfloat16)
+
+
+def row_picker():
+    picks = np.zeros((2, 4, 4 * PIX, 4, 128), np.float32)
+    for core in range(2):
+        base = PIX * core
+        for t in range(4):
+            for x in range(PIX):
+                at = 2 * x + t
+                out = x if core == 1 else 96 + x
+                if at == 0:
+                    slot, lane = 2, base + PIX - 1
+                elif at == 65:
+                    slot, lane = 3, base
+                else:
+                    slot, lane = (at - 1) // PIX, base + (at - 1) % PIX
+                picks[core, slot, lane, t, out] = 1
+    return picks.reshape(2, 512, 512).astype(ml_dtypes.bfloat16)
+
+
+def exchange_kernel(
+    n, tiles, grad, weight, edges, full, grad_full, weight_full, side, cap,
+    send_own, recv_own, send_side, recv_side, send_cap, recv_cap,
+):
+    p = lax.axis_index("tile")
+    k = lax.axis_index("chan")
+    other = 1 - k
+    toward = 1 - 2 * k
+    barrier = pltpu.get_barrier_semaphore()
+
+    def at(step):
+        return lax.rem(p + step + n, n)
+
+    def greet(row, core):
+        pl.semaphore_signal(barrier, inc=1, device_id=(row, core), device_id_type=MESH)
+
+    greet(p, other)
+    for core in range(2):
+        for step in (-1, 1):
+            greet(at(step), core)
+        for step in (3, 4, 5):
+            greet(at(toward * step), core)
+    pl.semaphore_wait(barrier, 11)
+
+    def send(src, dst, send_sem, recv_sem, row, core):
+        copy = pltpu.make_async_remote_copy(
+            src_ref=src,
+            dst_ref=dst,
+            send_sem=send_sem,
+            recv_sem=recv_sem,
+            device_id=(row, core),
+            device_id_type=MESH,
+        )
+        copy.start()
+        return copy
+
+    half = pl.ds(pl.multiple_of(64 * k, 64), 64)
+    wide = pl.ds(pl.multiple_of(128 * k, 128), 128)
+    copies = []
+    for g in range(2):
+        for s, step in ((0, 1), (1, -1)):
+            copies.append(
+                send(
+                    edges.at[g, 1 - s], side.at[s, :, half],
+                    send_side.at[g, s], recv_side.at[s, k], at(step), g,
+                )
+            )
+    for target, sign in ((1, 1), (0, -1)):
+        g = 1 - target
+        copies.append(
+            send(
+                edges.at[g, :, target], cap.at[0:2, half],
+                send_cap.at[target, 0], recv_cap.at[0, k], at(4 * sign), target,
+            )
+        )
+        for slot, step, column in ((2, 5 if sign > 0 else -3, 1), (3, 3 if sign > 0 else -5, 0)):
+            copies.append(
+                send(
+                    edges.at[g, column, target], cap.at[slot, half],
+                    send_cap.at[target, slot - 1], recv_cap.at[slot - 1, k], at(step), target,
+                )
+            )
+    copies.append(send(tiles.at[other], full.at[:, half], send_own.at[0], recv_own.at[0], p, other))
+    copies.append(send(grad.at[other], grad_full.at[wide], send_own.at[1], recv_own.at[1], p, other))
+    copies.append(send(weight, weight_full.at[k], send_own.at[2], recv_own.at[2], p, other))
+    full[:, half] = tiles[k]
+    grad_full[wide] = grad[k]
+    weight_full[k] = weight[...]
+    for copy in copies:
+        copy.wait_send()
+    copies[-1].wait_recv()
+    copies[-2].wait_recv()
+    copies[-3].wait_recv()
+
+    def arrived(dst, recv_sem):
+        pltpu.make_async_remote_copy(
+            src_ref=dst,
+            dst_ref=dst,
+            send_sem=send_own.at[0],
+            recv_sem=recv_sem,
+            device_id=(p, other),
+            device_id_type=MESH,
+        ).wait_recv()
+
+    for core in range(2):
+        part = pl.ds(64 * core, 64)
+        for s in range(2):
+            arrived(side.at[s, :, part], recv_side.at[s, core])
+        arrived(cap.at[0:2, part], recv_cap.at[0, core])
+        arrived(cap.at[2, part], recv_cap.at[1, core])
+        arrived(cap.at[3, part], recv_cap.at[2, core])
+
+
+def exchange(tiles, grad, weight, edges, n):
+    bf = jnp.bfloat16
+    vmem = pl.BlockSpec(memory_space=pltpu.VMEM)
+    return pl.pallas_call(
+        lambda *refs: exchange_kernel(n, *refs),
+        name="exchange",
+        out_shape=(
+            jax.ShapeDtypeStruct((4, 128, 1024), bf),
+            jax.ShapeDtypeStruct((256, 1024), bf),
+            jax.ShapeDtypeStruct((2, 9, 64, 128), bf),
+            jax.ShapeDtypeStruct((2, 2, 128, 128), bf),
+            jax.ShapeDtypeStruct((4, 128, 128), bf),
+        ),
+        in_specs=[vmem] * 4,
+        out_specs=(vmem,) * 5,
+        scratch_shapes=[
+            pltpu.SemaphoreType.DMA((3,)),
+            pltpu.SemaphoreType.DMA((3,)),
+            pltpu.SemaphoreType.DMA((2, 2)),
+            pltpu.SemaphoreType.DMA((2, 2)),
+            pltpu.SemaphoreType.DMA((2, 3)),
+            pltpu.SemaphoreType.DMA((3, 2)),
+        ],
+        compiler_params=pltpu.CompilerParams(
+            collective_id=1, has_side_effects=True, vmem_limit_bytes=32 << 20
+        ),
+    )(tiles, grad, weight, edges)
+
+
+def dot(a, b):
+    return jnp.dot(a, b, preferred_element_type=jnp.float32)
+
+
+def dot_lanes(a, b):
+    return lax.dot_general(a, b, (((1,), (1,)), ((), ())), preferred_element_type=jnp.float32)
+
+
+def group_kernel(
+    known, full, grad, weight, side, cap, flags, mix, mix_turned, phases, columns, rows,
+    merged, parts,
+    phase, lr, taps, wide_weight, hidden, dpre, conv_sum,
+):
+    bf = jnp.bfloat16
+    for ty in range(2):
+        for j in range(4):
+            lanes = pl.ds(256 * j, 256)
+            picked = dot(full[ty, :, lanes], phases[:256]) + dot(full[2 + ty, :, lanes], phases[256:])
+            out = pl.ds((4 * ty + j) * 128, 128)
+            for q in range(4):
+                phase[q, :, out] = picked[:, 128 * q : 128 * q + 128]
+    zero = jnp.zeros((), bf)
+    left = [jnp.where(known[0] >= 0, side[0, ty], zero) for ty in range(2)]
+    right = [jnp.where(known[1] >= 0, side[1, ty], zero) for ty in range(2)]
+    for ty in range(2):
+        picked = dot(left[ty], columns[:128]) + dot(right[ty], columns[128:])
+        for r in range(2):
+            lr[r, :, pl.ds(512 * ty, 512)] = picked[:, 512 * r : 512 * r + 512]
+    rim = jnp.zeros((128, 512), jnp.float32)
+    for slot, entry in enumerate((2, 2, 3, 4)):
+        rim += dot(jnp.where(known[entry] >= 0, cap[slot], zero), rows[128 * slot : 128 * slot + 128])
+    lane = lax.broadcasted_iota(jnp.int32, (128, 1024), 1)
+    first = (lane % 32) == 0
+    final = (lane % 32) == 31
+    narrow = lax.broadcasted_iota(jnp.int32, (128, 128), 1)
+    for tx in range(4):
+        for r in range(2):
+            if tx == 0:
+                base = jnp.where(first, lr[r], pltpu.roll(phase[2 * r + 1], 1, 1))
+            elif tx == 1:
+                base = phase[2 * r]
+            elif tx == 2:
+                base = phase[2 * r + 1]
+            else:
+                base = jnp.where(final, lr[r], pltpu.roll(phase[2 * r], 1023, 1))
+            taps[pl.ds(((1 + r) * 4 + tx) * 128, 128), :] = base.astype(bf)
+            corner = rim[:, 128 * tx : 128 * tx + 128]
+            if r == 1:
+                moved = pltpu.roll(base, 32, 1)
+                at = pl.ds(tx * 128, 128)
+                taps[at, 128:] = moved[:, 128:].astype(bf)
+                taps[at, :128] = jnp.where(narrow < 32, corner, moved[:, :128]).astype(bf)
+            else:
+                moved = pltpu.roll(base, 992, 1)
+                at = pl.ds((12 + tx) * 128, 128)
+                taps[at, :896] = moved[:, :896].astype(bf)
+                taps[at, 896:] = jnp.where(narrow >= 96, corner, moved[:, 896:]).astype(bf)
+    for b in range(2):
+        for i in range(3):
+            blank = pl.ds((4 * i + (3 if b == 0 else 0)) * 128, 128)
+            wide_weight[pl.ds(128 * b, 128), blank] = jnp.zeros((128, 128), bf)
+            for j in range(3):
+                for core in range(2):
+                    wide_weight[pl.ds(128 * b + 64 * core, 64), pl.ds((4 * i + j + b) * 128, 128)] = (
+                        weight[core, 3 * i + j]
+                    )
+    for a in range(2):
+        at = pl.ds(256 * a, 256)
+        pre = dot(wide_weight[...], taps[pl.ds(512 * a, 1536), :])
+        kept = (jnp.maximum(pre, 0.0) * flags[...]).astype(bf)
+        hidden[at, :] = kept
+        upstream = dot(mix[at, :], grad[...])
+        dpre[at, :] = jnp.where(kept.astype(jnp.float32) > 0, upstream, 0.0).astype(bf)
+    for h in range(2):
+        merged[h] = dot(mix_turned[pl.ds(128 * h, 128), :], hidden[...]).astype(bf)
+    for i in range(3):
+        strip = jnp.zeros((256, 512), jnp.float32)
+        for a in range(2):
+            strip += dot_lanes(dpre[pl.ds(256 * a, 256), :], taps[pl.ds(512 * (a + i), 512), :])
+        for j in range(3):
+            conv_sum[pl.ds((3 * i + j) * 128, 128), :] = (
+                strip[:128, 128 * j : 128 * j + 128] + strip[128:, 128 * j + 128 : 128 * j + 256]
+            )
+    for piece in range(32):
+        parts[piece, 0:36] = conv_sum[pl.ds(36 * piece, 36), :]
+        parts[piece, 36:48] = jnp.zeros((12, 128), jnp.float32)
+    mixed = dot_lanes(hidden[...], grad[...])
+    for piece in range(32):
+        parts[piece, 48:64] = mixed[16 * piece : 16 * piece + 16, :128]
+        parts[piece, 64:80] = mixed[16 * piece : 16 * piece + 16, 128:]
+
+
+def group_step(known, *arrays):
+    bf, f32 = jnp.bfloat16, jnp.float32
+    vmem = pl.BlockSpec(memory_space=pltpu.VMEM)
+    return pl.pallas_call(
+        group_kernel,
+        name="group_step",
+        out_shape=(
+            jax.ShapeDtypeStruct((2, 128, 1024), bf),
+            jax.ShapeDtypeStruct((32, 80, 128), f32),
+        ),
+        in_specs=[pl.BlockSpec(memory_space=pltpu.SMEM)] + [vmem] * len(arrays),
+        out_specs=(vmem, vmem),
+        scratch_shapes=[
+            pltpu.VMEM((4, 128, 1024), f32),
+            pltpu.VMEM((2, 128, 1024), f32),
+            pltpu.VMEM((2048, 1024), bf),
+            pltpu.VMEM((256, 1536), bf),
+            pltpu.VMEM((512, 1024), bf),
+            pltpu.VMEM((512, 1024), bf),
+            pltpu.VMEM((1152, 128), f32),
+        ],
+        compiler_params=pltpu.CompilerParams(vmem_limit_bytes=48 << 20),
+    )(known, *arrays)
+
+
+def finish_kernel(
+    n, part_ref, mine_ref, out_ref, merged_ref, near, held, recv,
+    send_a, recv_a, send_b, recv_b, send_c, recv_c, chip_send, chip_recv,
+):
+    me = lax.axis_index("tile")
+    core = lax.axis_index("chan")
+    other = 1 - core
+    barrier = pltpu.get_barrier_semaphore()
+
+    def remote(src, dst, send_sem, recv_sem, row, column):
+        copy = pltpu.make_async_remote_copy(
+            src_ref=src,
+            dst_ref=dst,
+            send_sem=send_sem,
+            recv_sem=recv_sem,
+            device_id=(row, column),
+            device_id_type=MESH,
+        )
+        copy.start()
+        return copy
+
+    for d in range(1, n):
+        pl.semaphore_signal(
+            barrier, inc=1, device_id=(lax.rem(me + d, n), core), device_id_type=MESH
+        )
+    pl.semaphore_signal(barrier, inc=1, device_id=(me, other), device_id_type=MESH)
+    held[...] = part_ref[other].astype(held.dtype)
+    pl.semaphore_wait(barrier, n)
+
+    over = remote(held, near, chip_send.at[0], chip_recv.at[0], me, other)
+    swap = remote(
+        mine_ref.at[other], merged_ref.at[core], chip_send.at[1], chip_recv.at[1], me, other
+    )
+    merged_ref[core] = mine_ref[core]
+    over.wait()
+    held[...] = (part_ref[core] + near[...].astype(jnp.float32)).astype(held.dtype)
+
+    scatter = []
+    for d in range(1, n):
+        peer = lax.rem(me + d, n)
+        scatter.append(remote(held.at[peer], recv.at[d], send_a.at[d], recv_a.at[d], peer, core))
+    total = part_ref[core, me] + near[me].astype(jnp.float32)
+    for d in range(1, n):
+        scatter[d - 1].wait_recv()
+        total += recv[d].astype(jnp.float32)
+    out_ref[core, me] = total.astype(out_ref.dtype)
+
+    spread = []
+    for d in range(1, n):
+        own = out_ref.at[core, me]
+        spread.append(remote(own, own, send_b.at[d], recv_b.at[d], lax.rem(me + d, n), core))
+    for copy in spread:
+        copy.wait_recv()
+    crossing = remote(out_ref.at[core], out_ref.at[core], send_c.at[0], recv_c.at[0], me, other)
+    for copy in scatter + spread:
+        copy.wait_send()
+    swap.wait()
+    crossing.wait()
+
+
+def finish(parts, mine, n):
+    bf = jnp.bfloat16
+    rows = parts.shape[2]
+    vmem = pl.BlockSpec(memory_space=pltpu.VMEM)
+    return pl.pallas_call(
+        lambda *refs: finish_kernel(n, *refs),
+        name="finish",
+        out_shape=(
+            jax.ShapeDtypeStruct((2, n, rows, LANES), bf),
+            jax.ShapeDtypeStruct(mine.shape, bf),
+        ),
+        in_specs=[vmem] * 2,
+        out_specs=(vmem, vmem),
+        scratch_shapes=[pltpu.VMEM((n, rows, LANES), bf)] * 3
+        + [pltpu.SemaphoreType.DMA((n,))] * 4
+        + [pltpu.SemaphoreType.DMA((1,))] * 2
+        + [pltpu.SemaphoreType.DMA((2,))] * 2,
+        compiler_params=pltpu.CompilerParams(
+            collective_id=2, has_side_effects=True, vmem_limit_bytes=32 << 20
+        ),
+    )(parts, mine)
+
+
+def group_per_core(
+    tile_features, conv_weight, merge_weight, tissue, group_tiles, neighbours, merged_grad
+):
+    bf = jnp.bfloat16
+    n = lax.axis_size("tile")
+    core = lax.axis_index("chan")
+    local = group_tiles % tile_features.shape[0]
+    order = local.reshape(2, 2, 2).transpose(0, 2, 1).reshape(-1)
+    ordered = jnp.take(tile_features, order, axis=0)
+    edges = jnp.einsum(
+        "tcp,pe->tce", ordered, jnp.asarray(edge_picker()), preferred_element_type=jnp.float32
+    ).astype(bf)
+    full, grad_full, weight_full, side, cap = exchange(
+        ordered.reshape(2, 4, 64, 1024),
+        merged_grad,
+        conv_weight.transpose(2, 3, 0, 1).reshape(9, 64, 128),
+        edges.reshape(2, 2, 2, 64, 128),
+        n,
+    )
+    known = lax.dynamic_index_in_dim(neighbours, core, 0, keepdims=False)
+    upper = jnp.stack([known[2], known[3], known[0], known[4], known[5]])
+    lower = jnp.stack([known[2], known[3], known[1], known[6], known[7]])
+    entries = jnp.where(core == 1, upper, lower)
+    mine = lax.dynamic_index_in_dim(local, core, 0, keepdims=False)
+    flags = jnp.take(tissue, mine).astype(jnp.float32).reshape(2, 1, 2, 1)
+    flags = jnp.broadcast_to(flags, (2, 16, 2, 16)).reshape(1, 1024)
+    mix = merge_weight.transpose(1, 0, 2).reshape(512, 256)
+    row_picks = lax.dynamic_index_in_dim(jnp.asarray(row_picker()), core, 0, keepdims=False)
+    merged_all, parts = group_step(
+        entries, full, grad_full, weight_full, side, cap, flags, mix, mix.T,
+        jnp.asarray(phase_picker()), jnp.asarray(column_picker()), row_picks,
+    )
+    summed, merged = finish(parts.reshape(2, n, 80, LANES), merged_all, n)
+    summed = summed.reshape(32, 80, LANES)
+    grad_conv = summed[:, :36].reshape(3, 3, 128, 128).transpose(2, 3, 0, 1).astype(jnp.float32)
+    grad_merge = (
+        summed[:, 48:].reshape(4, 8, 2, 16, LANES).transpose(0, 1, 3, 2, 4)
+        .reshape(4, 128, 256).transpose(1, 0, 2).astype(jnp.float32)
+    )
+    return merged, grad_conv, grad_merge
+
+
 def solution(mesh):
     placed = (
         P("tile", "chan", None),
@@ -260,8 +672,9 @@
         P("tile", None),
         P("tile", "chan", None),
     )
+    pairs = mesh.shape["chan"] == 2 and mesh.shape["tile"] == 16
     return jax.shard_map(
-        shards,
+        group_per_core if pairs else shards,
         mesh=mesh,
         in_specs=placed,
         out_specs=(P("tile", "chan", None), P(), P()),

time: 139 us -> 61.4 us (0.44)
  matrix products: 32.5 us -> 0.47 us
  Pallas kernels: 22.3 us -> 41.8 us
  local copies, waits for them, and re-layouts: 31 us -> 16.6 us
  starting transfers between devices: 13.3 us -> 0 us
  between operations: 14.1 us -> 0.83 us
  waiting for transfers between devices: 10.8 us -> 0 us
  other arithmetic: 11.3 us -> 0.96 us
  blocking collectives: 2.17 us -> 0 us
    pallas_call x1 -> x3, Pallas kernels: 22.3 us -> 41.8 us  [the longest x1 22.7 us: finish(): pl.pallas_call(lambda *refs: finish_kernel(n, *refs), name='finish', out_...]
    another operation x1 -> x0, matrix products: 15.8 us -> none  [shards(): conv_rows = conv_term.transpose(2, 3, 0, 1).reshape(-1, LANES)]
    ppermute x8 -> x0, starting transfers between devices: 13.2 us -> none  [passed_along(): return lax.ppermute(block, axis, route)]
    conv_general_dilated x1 -> x0, matrix products: 11.9 us -> none  [shards(): lax.conv_general_dilated(padded, conv_weight, (1, 1), 'VALID', dimension_...]
    ppermute x8 -> x0, waiting for transfers between devices: 10 us -> none  [passed_along(): return lax.ppermute(block, axis, route)]
    transpose x5 -> x2, local copies, waits for them, and re-layouts: 10.9 us -> 1.31 us  [the longest x1 1.21 us: group_per_core(): mix = merge_weight.transpose(1, 0, 2).reshape(512, 256)]
    gather x6 -> x3, local copies, waits for them, and re-layouts: 10.2 us -> 1.99 us  [the longest x2 1.38 us: group_per_core(): flags = jnp.take(tissue, mine).astype(jnp.float32).reshape(2, 1, 2, 1)]
    concatenate x2 -> x0, other arithmetic: 7.99 us -> none  [the longest x1 7.25 us: framed(): jnp.concatenate([upper[:, :, None, :], middle, lower[:, :, None, :]], axi...]
  transfers between devices with their start and end apart: 11 -> 0, of which waited for: 2 -> 0; matrix products, arithmetic and copies ran while one was open for 51% -> 0% of each run, Pallas kernels for 16% -> 0%
where the time goes in v2:
time: 61.4 us; the launch traced here: 60.7 us
  Pallas kernels  41.8 us (68%)
  local copies, waits for them, and re-layouts  16.6 us (27%)
  other arithmetic  0.96 us (2%)
  between operations  0.83 us (1%)
    pallas_call x1, Pallas kernels, finish(): pl.pallas_call(lambda *refs: finish_kernel(n, *refs), name='finish', out_...  22.7 us
    pallas_call x1, Pallas kernels, exchange(): pl.pallas_call(lambda *refs: exchange_kernel(n, *refs), name='exchange',...  12.8 us
    pallas_call x1, Pallas kernels, group_step(): pl.pallas_call(group_kernel, name='group_step', out_shape=(jax.ShapeDtype...  6.42 us
    another operation x1, local copies, waits for them, and re-layouts, group_per_core(): lower = jnp.stack([known[2], known[3], known[1], known[6], known[7]])  3.28 us
    another operation x1, local copies, waits for them, and re-layouts, group_per_core(): upper = jnp.stack([known[2], known[3], known[0], known[4], known[5]])  3.27 us
    unnamed x16, local copies, waits for them, and re-layouts  2.06 us
    convert_element_type x2, local copies, waits for them, and re-layouts, group_per_core(): grad_merge = summed[:, 48:].reshape(4, 8, 2, 16, LANES).transpose(0, 1, 3...  1.51 us
    gather x2, local copies, waits for them, and re-layouts, group_per_core(): flags = jnp.take(tissue, mine).astype(jnp.float32).reshape(2, 1, 2, 1)  1.38 us

profile of v2, /device:TPU:0, one launch (start us, length us, event | category | flops | bytes accessed | tf_op | source)
XLA Modules:
  0.0 60.7 jit_solution(12282286745949935346)
XLA Ops:
  0.6 0.0 copy-start
  0.6 0.0 copy-start.5
  0.7 0.8 %constant_dynamic-slice_fusion.1 = s32[1,8]{1,0:T(1,128)S(1)} fusion(s32[2,8]{1,0:T(2,128)} %param.16, s32[]{:T(128)S(6)} %select_n.78), kind=kLoop, calls=%fused_computation.28 | loop fusion | bytes 68 | tf_op jit(solution)/shard_map/jit(dynamic_index_in_dim)/dynamic_slice | solution.py:642
  1.5 0.7 %and_select_fusion.1 = s32[2,4]{1,0:T(2,128)S(1)} fusion(s32[2,4]{1,0:T(2,128)} %param.15), kind=kLoop, calls=%fused_computation.23 | loop fusion | flops 88 | bytes 64 | tf_op jit(solution)/shard_map/jit(remainder)/select_n | solution.py:629
  2.2 0.1 squeeze.12
  2.3 0.1 reshape.146
  2.4 0.1 copy.20
  2.5 0.1 reshape.150
  2.6 0.1 reshape.148
  2.7 0.1 reshape.147
  2.8 1.3 %gather_fusion.1 = s32[4]{0:T(128)S(1)} fusion(s32[8]{0:T(128)} %param.14, s32[1024]{0:T(1024)S(1)} %pad_clamp_fusion), kind=kCustom, calls=%fused_computation.1 | custom fusion | bytes 48 | tf_op jit(solution)/shard_map/jit(_take)/gather | solution.py:647
  4.1 0.1 gather.15
  4.2 0.7 %fusion.10 = (s32[1,1]{1,0:T(1,128)}, s32[1,1]{1,0:T(1,128)}, s32[1,1]{1,0:T(1,128)}, s32[1,1]{1,0:T(1,128)}, s32[1,1]{1,0:T(1,128)}, /*index=5*/s32[1,1]{1,0:T(1,128)}, s32[1,1]{1,0:T(1,128)}, s32[1,1]{1,0:T(1,128)}) fusion(s32[1,8]{1,0:T(1,128)S(1)} %constant_dynamic-slice_fusion.1), kind=kLoop, calls=%fused_computation.34 | loop fusion | bytes 64 | tf_op jit(solution)/shard_map/slice | solution.py:644
  4.8 3.3 %stack.7 = s32[5]{0:T(128)S(1)} concatenate(s32[1]{0:T(128)} %bitcast, s32[1]{0:T(128)} %bitcast.1, s32[1]{0:T(128)} %bitcast.5, s32[1]{0:T(128)} %bitcast.6, s32[1]{0:T(128)} %bitcast.7), dimensions={0} | concatenate | bytes 40 | tf_op jit(solution)/shard_map/stack | solution.py:644
  8.1 3.3 %stack.6 = s32[5]{0:T(128)S(1)} concatenate(s32[1]{0:T(128)} %bitcast, s32[1]{0:T(128)} %bitcast.1, s32[1]{0:T(128)} %bitcast.2, s32[1]{0:T(128)} %bitcast.3, s32[1]{0:T(128)} %bitcast.4), dimensions={0} | concatenate | bytes 40 | tf_op jit(solution)/shard_map/stack | solution.py:643
  11.4 0.1 broadcast_in_dim.25
  11.5 0.1 reshape.152.flags
  11.6 1.2 %copy.23 = bf16[4,128,256]{1,0,2:T(4,128)(2,1)S(1)} copy(bf16[4,128,256]{2,0,1:T(4,128)(2,1)} %bitcast.60) | data formatting | bytes 524288 | tf_op jit(solution)/shard_map/transpose | solution.py:649
  12.9 0.1 copy.24.mix
  13.1 0.6 %gather_fusion = bf16[8,64,1024]{2,1,0:T(8,128)(2,1)S(1)} fusion(bf16[8,64,1024]{2,1,0:T(8,128)(2,1)S(1)} %copy-done, s32[1024]{0:T(1024)S(1)} %pad_clamp_fusion.1), kind=kCustom, calls=%fused_computation | custom fusion | bytes 2097184 | tf_op jit(solution)/shard_map/jit(_take)/gather | solution.py:631
  13.7 0.3 copy-done.6
  14.0 0.5 convolution_convert_fusion
  14.5 0.2 broadcast_select_fusion.refs_0_
  14.7 0.9 %copy-done.1 = bf16[2,128,1024]{2,1,0:T(8,128)(2,1)S(1)} copy-done((bf16[2,128,1024]{2,1,0:T(8,128)(2,1)S(1)}, bf16[2,128,1024]{2,1,0:T(8,128)(2,1)}, u32[]{:S(2)}) %copy-start.1) | copy-done | bytes 524312
  15.6 0.0 copy-done.4
  15.6 12.8 %exchange.1 = (bf16[4,128,1024]{2,1,0:T(8,128)(2,1)S(1)}, bf16[256,1024]{1,0:T(8,128)(2,1)S(1)}, bf16[2,9,64,128]{3,2,1,0:T(8,128)(2,1)S(1)}, bf16[2,2,128,128]{...) custom-call(bf16[2,4,64,1024]{3,2,1,0:T(8,128)(2,1)S(1)} %broadcast_select_fusion.refs_0_, bf16[2,128,1024]{2,1,0:T(8,128)(2,1)S(1)} %copy-done.1, ...), custom_call_target="tpu_custom_call" | custom-call | tf_op jit(solution)/shard_map/exchange/pallas_call | solution.py:397
  28.4 6.4 %group_step.1 = (bf16[2,128,1024]{2,1,0:T(8,128)(2,1)S(1)}, f32[32,80,128]{2,1,0:T(8,128)S(1)}) custom-call(s32[5]{0:T(128)S(1)} %broadcast_select_fusion.1.known, bf16[4,128,1024]{2,1,0:T(8,128)(2,1)S(1)} %get-tuple-element.12.full, bf16[256,1024]{1,0:T(8,128)(2,1)S(1)} %get-tuple-element.13.grad, bf16[2,9,64,128]{3,2,1,0:T(8,128)(2,1)S(1)} %get-tuple-element.14.weight, ...), custom_call_target="tpu_custom_call" | custom-call | tf_op jit(solution)/shard_map/group_step/pallas_call | solution.py:518
  34.8 22.7 %finish.1 = (bf16[2,16,80,128]{3,2,1,0:T(8,128)(2,1)S(1)}, bf16[2,128,1024]{2,1,0:T(8,128)(2,1)S(1)}) custom-call(f32[2,16,80,128]{3,2,1,0:T(8,128)S(1)} %bitcast.49, bf16[2,128,1024]{2,1,0:T(8,128)(2,1)S(1)} %get-tuple-element.18.refs_1_), custom_call_target="tpu_custom_call" | custom-call | tf_op jit(solution)/shard_map/finish/pallas_call | solution.py:604
  57.6 0.9 %reshape.156 = f32[3,3,128,128]{3,2,1,0:T(8,128)} reshape(f32[32,36,128]{2,1,0:T(8,128)S(1)} %slice_convert_fusion) | data formatting | bytes 1179648 | tf_op jit(solution)/shard_map/convert_element_type | solution.py:657
  58.4 0.2 copy.31
  58.6 1.3 %reshape.157 = f32[4,128,256]{2,0,1:T(4,128)} reshape(f32[4,8,16,2,128]{4,3,0,2,1:T(2,128)S(1)} %bitcast.55) | data formatting | bytes 1048576 | tf_op jit(solution)/shard_map/convert_element_type | solution.py:660
  59.9 0.8 %copy.34 = bf16[2,128,1024]{2,1,0:T(8,128)(2,1)} copy(bf16[2,128,1024]{2,1,0:T(8,128)(2,1)S(1)} %get-tuple-element.34) | data formatting | bytes 1048576
  (22 shorter events, 0.3 us)
Async XLA Ops:
  0.6 12.4 %copy-start = (bf16[8,64,1024]{2,1,0:T(8,128)(2,1)S(1)}, bf16[8,64,1024]{2,1,0:T(8,128)(2,1)}, u32[]{:S(2)}) copy-start(bf16[8,64,1024]{2,1,0:T(8,128)(2,1)} %param.11) | copy-start | bytes 3145732
  0.6 12.4 %copy-start.5 = (bf16[2,512,512]{2,1,0:T(8,128)(2,1)S(1)}, bf16[2,512,512]{2,1,0:T(8,128)(2,1)}, u32[]{:S(2)}) copy-start(bf16[2,512,512]{2,1,0:T(8,128)(2,1)} %constant.69.clone) | copy-start | bytes 3145732
  13.1 1.0 %copy-start.6 = (bf16[1024,128,1]{1,0,2:T(8,128)(2,1)S(1)}, bf16[1024,128,1]{1,0,2:T(8,128)(2,1)}, u32[]{:S(2)}) copy-start(bf16[1024,128,1]{1,0,2:T(8,128)(2,1)} %constant.77) | copy-start | bytes 786436
  14.5 1.0 %copy-start.1 = (bf16[2,128,1024]{2,1,0:T(8,128)(2,1)S(1)}, bf16[2,128,1024]{2,1,0:T(8,128)(2,1)}, u32[]{:S(2)}) copy-start(bf16[2,128,1024]{2,1,0:T(8,128)(2,1)} %refs_1_.1) | copy-start | bytes 1572868
  14.5 1.1 %copy-start.4 = (bf16[64,128,3,3]{1,0,3,2:T(8,128)(2,1)S(1)}, bf16[64,128,3,3]{1,0,3,2:T(8,128)(2,1)}, u32[]{:S(2)}) copy-start(bf16[64,128,3,3]{1,0,3,2:T(8,128)(2,1)} %param.12) | copy-start | bytes 442372
  15.6 12.8 %copy-start.2 = (bf16[256,1024]{1,0:T(8,128)(2,1)S(1)}, bf16[256,1024]{1,0:T(8,128)(2,1)}, u32[]{:S(2)}) copy-start(bf16[256,1024]{1,0:T(8,128)(2,1)} %constant.71.clone.columns) | copy-start | bytes 1572868
  15.6 12.8 %copy-start.3 = (bf16[512,512]{1,0:T(8,128)(2,1)S(1)}, bf16[512,512]{1,0:T(8,128)(2,1)}, u32[]{:S(2)}) copy-start(bf16[512,512]{1,0:T(8,128)(2,1)} %constant.70.clone.phases) | copy-start | bytes 1572868

commit v3 on v2

--- a/solution.py
+++ b/solution.py
@@ -299,8 +299,8 @@
 
 
 def exchange_kernel(
-    n, tiles, grad, weight, edges, full, grad_full, weight_full, side, cap,
-    send_own, recv_own, send_side, recv_side, send_cap, recv_cap,
+    n, ids, stored, grad, weight, picks, full, grad_full, weight_full, side, cap,
+    tiles, sides, caps, corners, send_own, recv_own, send_side, recv_side, send_cap, recv_cap,
 ):
     p = lax.axis_index("tile")
     k = lax.axis_index("chan")
@@ -320,6 +320,35 @@
             greet(at(step), core)
         for step in (3, 4, 5):
             greet(at(toward * step), core)
+    count = stored.shape[0]
+    for g in range(2):
+        for column in range(2):
+            for row in range(2):
+                tiles[g, 2 * column + row] = stored[lax.rem(ids[g, 2 * row + column], count)]
+    edge = dot(tiles[...].reshape(512, 1024), picks[...])
+    lane = lax.broadcasted_iota(jnp.int32, (64, 128), 1)
+
+    def edge_of(g, column, row):
+        start = 64 * (4 * g + 2 * column + row)
+        return edge[start : start + 64]
+
+    bf = jnp.bfloat16
+    for g in range(2):
+        sides[g, 0] = jnp.where(
+            lane < 96, edge_of(g, 0, 0), pltpu.roll(edge_of(g, 0, 1), 32, 1)
+        ).astype(bf)
+        sides[g, 1] = jnp.where(
+            lane >= 96, edge_of(g, 1, 0), pltpu.roll(edge_of(g, 1, 1), 96, 1)
+        ).astype(bf)
+    for target in range(2):
+        g = 1 - target
+        caps[target] = jnp.where(
+            lane < 32 + 32 * target,
+            edge_of(g, 0, target),
+            pltpu.roll(edge_of(g, 1, target), 32, 1),
+        ).astype(bf)
+        for column in range(2):
+            corners[target, column] = edge_of(g, column, target).astype(bf)
     pl.semaphore_wait(barrier, 11)
 
     def send(src, dst, send_sem, recv_sem, row, core):
@@ -341,23 +370,22 @@
         for s, step in ((0, 1), (1, -1)):
             copies.append(
                 send(
-                    edges.at[g, 1 - s], side.at[s, :, half],
+                    sides.at[g, 1 - s], side.at[s, half],
                     send_side.at[g, s], recv_side.at[s, k], at(step), g,
                 )
             )
     for target, sign in ((1, 1), (0, -1)):
-        g = 1 - target
         copies.append(
             send(
-                edges.at[g, :, target], cap.at[0:2, half],
+                caps.at[target], cap.at[0, half],
                 send_cap.at[target, 0], recv_cap.at[0, k], at(4 * sign), target,
             )
         )
-        for slot, step, column in ((2, 5 if sign > 0 else -3, 1), (3, 3 if sign > 0 else -5, 0)):
+        for slot, step, column in ((1, 5 if sign > 0 else -3, 1), (2, 3 if sign > 0 else -5, 0)):
             copies.append(
                 send(
-                    edges.at[g, column, target], cap.at[slot, half],
-                    send_cap.at[target, slot - 1], recv_cap.at[slot - 1, k], at(step), target,
+                    corners.at[target, column], cap.at[slot, half],
+                    send_cap.at[target, slot], recv_cap.at[slot, k], at(step), target,
                 )
             )
     copies.append(send(tiles.at[other], full.at[:, half], send_own.at[0], recv_own.at[0], p, other))
@@ -385,13 +413,12 @@
     for core in range(2):
         part = pl.ds(64 * core, 64)
         for s in range(2):
-            arrived(side.at[s, :, part], recv_side.at[s, core])
-        arrived(cap.at[0:2, part], recv_cap.at[0, core])
-        arrived(cap.at[2, part], recv_cap.at[1, core])
-        arrived(cap.at[3, part], recv_cap.at[2, core])
-
-
-def exchange(tiles, grad, weight, edges, n):
+            arrived(side.at[s, part], recv_side.at[s, core])
+        for slot in range(3):
+            arrived(cap.at[slot, part], recv_cap.at[slot, core])
+
+
+def exchange(ids, tiles, grad, weight, picks, n):
     bf = jnp.bfloat16
     vmem = pl.BlockSpec(memory_space=pltpu.VMEM)
     return pl.pallas_call(
@@ -401,12 +428,16 @@
             jax.ShapeDtypeStruct((4, 128, 1024), bf),
             jax.ShapeDtypeStruct((256, 1024), bf),
             jax.ShapeDtypeStruct((2, 9, 64, 128), bf),
-            jax.ShapeDtypeStruct((2, 2, 128, 128), bf),
-            jax.ShapeDtypeStruct((4, 128, 128), bf),
+            jax.ShapeDtypeStruct((2, 128, 128), bf),
+            jax.ShapeDtypeStruct((3, 128, 128), bf),
         ),
-        in_specs=[vmem] * 4,
+        in_specs=[pl.BlockSpec(memory_space=pltpu.SMEM)] + [vmem] * 4,
         out_specs=(vmem,) * 5,
         scratch_shapes=[
+            pltpu.VMEM((2, 4, 64, 1024), bf),
+            pltpu.VMEM((2, 2, 64, 128), bf),
+            pltpu.VMEM((2, 64, 128), bf),
+            pltpu.VMEM((2, 2, 64, 128), bf),
             pltpu.SemaphoreType.DMA((3,)),
             pltpu.SemaphoreType.DMA((3,)),
             pltpu.SemaphoreType.DMA((2, 2)),
@@ -417,7 +448,7 @@
         compiler_params=pltpu.CompilerParams(
             collective_id=1, has_side_effects=True, vmem_limit_bytes=32 << 20
         ),
-    )(tiles, grad, weight, edges)
+    )(ids, tiles, grad, weight, picks)
 
 
 def dot(a, b):
@@ -429,11 +460,21 @@
 
 
 def group_kernel(
-    known, full, grad, weight, side, cap, flags, mix, mix_turned, phases, columns, rows,
+    near_groups, ids, tissue, full, grad, weight, side, cap, mix, mix_turned, phases, columns, rows,
     merged, parts,
     phase, lr, taps, wide_weight, hidden, dpre, conv_sum,
 ):
     bf = jnp.bfloat16
+    core = lax.axis_index("chan")
+    count = tissue.shape[0]
+    entry_of = (2, 3, core * -1 + 1, core * -2 + 6, core * -2 + 7)
+    known = [near_groups[core, entry] for entry in entry_of]
+    kinds = [tissue[lax.rem(ids[core, t], count)].astype(jnp.float32) for t in range(4)]
+    spot = lax.broadcasted_iota(jnp.int32, (1, 1024), 1)
+    east = (spot % 32) >= 16
+    flags = jnp.where(
+        spot >= 512, jnp.where(east, kinds[3], kinds[2]), jnp.where(east, kinds[1], kinds[0])
+    )
     for ty in range(2):
         for j in range(4):
             lanes = pl.ds(256 * j, 256)
@@ -442,15 +483,25 @@
             for q in range(4):
                 phase[q, :, out] = picked[:, 128 * q : 128 * q + 128]
     zero = jnp.zeros((), bf)
-    left = [jnp.where(known[0] >= 0, side[0, ty], zero) for ty in range(2)]
-    right = [jnp.where(known[1] >= 0, side[1, ty], zero) for ty in range(2)]
+    blank_side = jnp.zeros((), jnp.float32)
+    near_left = jnp.where(known[0] >= 0, side[0].astype(jnp.float32), blank_side)
+    near_right = jnp.where(known[1] >= 0, side[1].astype(jnp.float32), blank_side)
+    near_cap = jnp.where(known[2] >= 0, cap[0].astype(jnp.float32), blank_side)
+    left = [near_left.astype(bf), pltpu.roll(near_left, 32, 1).astype(bf)]
+    right = [near_right.astype(bf), pltpu.roll(near_right, 96, 1).astype(bf)]
     for ty in range(2):
         picked = dot(left[ty], columns[:128]) + dot(right[ty], columns[128:])
         for r in range(2):
             lr[r, :, pl.ds(512 * ty, 512)] = picked[:, 512 * r : 512 * r + 512]
     rim = jnp.zeros((128, 512), jnp.float32)
-    for slot, entry in enumerate((2, 2, 3, 4)):
-        rim += dot(jnp.where(known[entry] >= 0, cap[slot], zero), rows[128 * slot : 128 * slot + 128])
+    row_sources = (
+        near_cap.astype(bf),
+        pltpu.roll(near_cap, 96, 1).astype(bf),
+        jnp.where(known[3] >= 0, cap[1], zero),
+        jnp.where(known[4] >= 0, cap[2], zero),
+    )
+    for slot, source in enumerate(row_sources):
+        rim += dot(source, rows[core, pl.ds(128 * slot, 128), :])
     lane = lax.broadcasted_iota(jnp.int32, (128, 1024), 1)
     first = (lane % 32) == 0
     final = (lane % 32) == 31
@@ -489,7 +540,7 @@
     for a in range(2):
         at = pl.ds(256 * a, 256)
         pre = dot(wide_weight[...], taps[pl.ds(512 * a, 1536), :])
-        kept = (jnp.maximum(pre, 0.0) * flags[...]).astype(bf)
+        kept = (jnp.maximum(pre, 0.0) * flags).astype(bf)
         hidden[at, :] = kept
         upstream = dot(mix[at, :], grad[...])
         dpre[at, :] = jnp.where(kept.astype(jnp.float32) > 0, upstream, 0.0).astype(bf)
@@ -512,7 +563,7 @@
         parts[piece, 64:80] = mixed[16 * piece : 16 * piece + 16, 128:]
 
 
-def group_step(known, *arrays):
+def group_step(near_groups, ids, tissue, *arrays):
     bf, f32 = jnp.bfloat16, jnp.float32
     vmem = pl.BlockSpec(memory_space=pltpu.VMEM)
     return pl.pallas_call(
@@ -522,7 +573,7 @@
             jax.ShapeDtypeStruct((2, 128, 1024), bf),
             jax.ShapeDtypeStruct((32, 80, 128), f32),
         ),
-        in_specs=[pl.BlockSpec(memory_space=pltpu.SMEM)] + [vmem] * len(arrays),
+        in_specs=[pl.BlockSpec(memory_space=pltpu.SMEM)] * 3 + [vmem] * len(arrays),
         out_specs=(vmem, vmem),
         scratch_shapes=[
             pltpu.VMEM((4, 128, 1024), f32),
@@ -534,11 +585,11 @@
             pltpu.VMEM((1152, 128), f32),
         ],
         compiler_params=pltpu.CompilerParams(vmem_limit_bytes=48 << 20),
-    )(known, *arrays)
+    )(near_groups, ids, tissue, *arrays)
 
 
 def finish_kernel(
-    n, part_ref, mine_ref, out_ref, merged_ref, near, held, recv,
+    n, part_ref, mine_ref, conv_ref, mix_ref, merged_ref, out_ref, near, held, recv,
     send_a, recv_a, send_b, recv_b, send_c, recv_c, chip_send, chip_recv,
 ):
     me = lax.axis_index("tile")
@@ -588,13 +639,22 @@
     for d in range(1, n):
         own = out_ref.at[core, me]
         spread.append(remote(own, own, send_b.at[d], recv_b.at[d], lax.rem(me + d, n), core))
-    for copy in spread:
-        copy.wait_recv()
-    crossing = remote(out_ref.at[core], out_ref.at[core], send_c.at[0], recv_c.at[0], me, other)
+    own = out_ref.at[core, me]
+    crossing = [remote(own, own, send_c.at[0], recv_c.at[0], me, other)]
+    for d in range(1, n):
+        spread[d - 1].wait_recv()
+        piece = out_ref.at[core, lax.rem(me + n - d, n)]
+        crossing.append(remote(piece, piece, send_c.at[d], recv_c.at[d], me, other))
     for copy in scatter + spread:
         copy.wait_send()
     swap.wait()
-    crossing.wait()
+    for copy in crossing:
+        copy.wait()
+    for piece in range(32):
+        block = out_ref[piece // n, piece % n].astype(jnp.float32)
+        conv_ref[pl.ds(36 * piece, 36), :] = block[:36]
+        mix_ref[pl.ds(16 * piece, 16), :128] = block[48:64]
+        mix_ref[pl.ds(16 * piece, 16), 128:] = block[64:]
 
 
 def finish(parts, mine, n):
@@ -605,14 +665,15 @@
         lambda *refs: finish_kernel(n, *refs),
         name="finish",
         out_shape=(
-            jax.ShapeDtypeStruct((2, n, rows, LANES), bf),
+            jax.ShapeDtypeStruct((1152, LANES), jnp.float32),
+            jax.ShapeDtypeStruct((512, 2 * LANES), jnp.float32),
             jax.ShapeDtypeStruct(mine.shape, bf),
         ),
         in_specs=[vmem] * 2,
-        out_specs=(vmem, vmem),
-        scratch_shapes=[pltpu.VMEM((n, rows, LANES), bf)] * 3
-        + [pltpu.SemaphoreType.DMA((n,))] * 4
-        + [pltpu.SemaphoreType.DMA((1,))] * 2
+        out_specs=(vmem, vmem, vmem),
+        scratch_shapes=[pltpu.VMEM((2, n, rows, LANES), bf)]
+        + [pltpu.VMEM((n, rows, LANES), bf)] * 3
+        + [pltpu.SemaphoreType.DMA((n,))] * 6
         + [pltpu.SemaphoreType.DMA((2,))] * 2,
         compiler_params=pltpu.CompilerParams(
             collective_id=2, has_side_effects=True, vmem_limit_bytes=32 << 20
@@ -623,42 +684,23 @@
 def group_per_core(
     tile_features, conv_weight, merge_weight, tissue, group_tiles, neighbours, merged_grad
 ):
-    bf = jnp.bfloat16
     n = lax.axis_size("tile")
-    core = lax.axis_index("chan")
-    local = group_tiles % tile_features.shape[0]
-    order = local.reshape(2, 2, 2).transpose(0, 2, 1).reshape(-1)
-    ordered = jnp.take(tile_features, order, axis=0)
-    edges = jnp.einsum(
-        "tcp,pe->tce", ordered, jnp.asarray(edge_picker()), preferred_element_type=jnp.float32
-    ).astype(bf)
     full, grad_full, weight_full, side, cap = exchange(
-        ordered.reshape(2, 4, 64, 1024),
+        group_tiles,
+        tile_features,
         merged_grad,
         conv_weight.transpose(2, 3, 0, 1).reshape(9, 64, 128),
-        edges.reshape(2, 2, 2, 64, 128),
+        jnp.asarray(edge_picker()),
         n,
     )
-    known = lax.dynamic_index_in_dim(neighbours, core, 0, keepdims=False)
-    upper = jnp.stack([known[2], known[3], known[0], known[4], known[5]])
-    lower = jnp.stack([known[2], known[3], known[1], known[6], known[7]])
-    entries = jnp.where(core == 1, upper, lower)
-    mine = lax.dynamic_index_in_dim(local, core, 0, keepdims=False)
-    flags = jnp.take(tissue, mine).astype(jnp.float32).reshape(2, 1, 2, 1)
-    flags = jnp.broadcast_to(flags, (2, 16, 2, 16)).reshape(1, 1024)
     mix = merge_weight.transpose(1, 0, 2).reshape(512, 256)
-    row_picks = lax.dynamic_index_in_dim(jnp.asarray(row_picker()), core, 0, keepdims=False)
     merged_all, parts = group_step(
-        entries, full, grad_full, weight_full, side, cap, flags, mix, mix.T,
-        jnp.asarray(phase_picker()), jnp.asarray(column_picker()), row_picks,
-    )
-    summed, merged = finish(parts.reshape(2, n, 80, LANES), merged_all, n)
-    summed = summed.reshape(32, 80, LANES)
-    grad_conv = summed[:, :36].reshape(3, 3, 128, 128).transpose(2, 3, 0, 1).astype(jnp.float32)
-    grad_merge = (
-        summed[:, 48:].reshape(4, 8, 2, 16, LANES).transpose(0, 1, 3, 2, 4)
-        .reshape(4, 128, 256).transpose(1, 0, 2).astype(jnp.float32)
-    )
+        neighbours, group_tiles, tissue, full, grad_full, weight_full, side, cap, mix, mix.T,
+        jnp.asarray(phase_picker()), jnp.asarray(column_picker()), jnp.asarray(row_picker()),
+    )
+    summed_conv, summed_mix, merged = finish(parts.reshape(2, n, 80, LANES), merged_all, n)
+    grad_conv = summed_conv.reshape(3, 3, 128, 128).transpose(2, 3, 0, 1)
+    grad_merge = summed_mix.reshape(4, 128, 256).transpose(1, 0, 2)
     return merged, grad_conv, grad_merge
 
 

time: 61.4 us -> 53 us (0.86)
  local copies, waits for them, and re-layouts: 16.6 us -> 9.24 us
  other arithmetic: 0.96 us -> 0 us
    another operation x2 -> x0, local copies, waits for them, and re-layouts: 6.55 us -> none  [the longest x1 3.28 us: group_per_core(): lower = jnp.stack([known[2], known[3], known[1], known[6], known[7]])]
    unnamed x16 -> x27, local copies, waits for them, and re-layouts: 2.06 us -> 6.66 us
    convert_element_type x3 -> x0, local copies, waits for them, and re-layouts: 2.36 us -> none  [the longest x2 1.51 us: group_per_core(): grad_merge = summed[:, 48:].reshape(4, 8, 2, 16, LANES).transpose(0, 1, 3...]
    gather x3 -> x0, local copies, waits for them, and re-layouts: 1.99 us -> none  [the longest x2 1.38 us: group_per_core(): flags = jnp.take(tissue, mine).astype(jnp.float32).reshape(2, 1, 2, 1)]
    pallas_call x1, Pallas kernels: 6.42 us -> 7.58 us  [group_step(): pl.pallas_call(group_kernel, name='group_step', out_shape=(jax.ShapeDtype...]
    select_n x5 -> x0, other arithmetic: 0.87 us -> none  [the longest x1 0.69 us: group_per_core(): local = group_tiles % tile_features.shape[0]]
    dynamic_slice x2 -> x0, local copies, waits for them, and re-layouts: 0.86 us -> none  [the longest x1 0.83 us: group_per_core(): known = lax.dynamic_index_in_dim(neighbours, core, 0, keepdims=False)]
    pallas_call x1, Pallas kernels: 12.8 us -> 12 us  [exchange(): pl.pallas_call(lambda *refs: exchange_kernel(n, *refs), name='exchange',...]
where the time goes in v3:
time: 53 us; the launch traced here: 52.4 us
  Pallas kernels  42.3 us (80%)
  local copies, waits for them, and re-layouts  9.24 us (17%)
  between operations  0.77 us (1%)
    pallas_call x1, Pallas kernels, finish(): pl.pallas_call(lambda *refs: finish_kernel(n, *refs), name='finish', out_...  22.8 us
    pallas_call x1, Pallas kernels, exchange(): pl.pallas_call(lambda *refs: exchange_kernel(n, *refs), name='exchange',...  12 us
    pallas_call x1, Pallas kernels, group_step(): pl.pallas_call(group_kernel, name='group_step', out_shape=(jax.ShapeDtype...  7.58 us
    unnamed x27, local copies, waits for them, and re-layouts  6.66 us
    transpose x1, local copies, waits for them, and re-layouts, group_per_core(): mix = merge_weight.transpose(1, 0, 2).reshape(512, 256)  1.32 us
    reshape x1, local copies, waits for them, and re-layouts, group_per_core(): grad_merge = summed_mix.reshape(4, 128, 256).transpose(1, 0, 2)  1.13 us

profile of v3, /device:TPU:0, one launch (start us, length us, event | category | flops | bytes accessed | tf_op | source)
XLA Modules:
  0.0 52.4 jit_solution(7036228630493454420)
XLA Ops:
  0.6 0.0 copy-start.3
  0.6 0.0 copy-start.1
  0.7 1.3 %copy.14 = bf16[4,128,256]{1,0,2:T(4,128)(2,1)S(1)} copy(bf16[4,128,256]{2,0,1:T(4,128)(2,1)} %bitcast.31) | data formatting | bytes 524288 | tf_op jit(solution)/shard_map/transpose | solution.py:696
  2.0 0.0 copy-start.2
  2.0 0.1 copy.15.mix
  2.2 0.0 copy-done.3
  2.2 0.0 copy-done.1
  2.2 0.0 copy-start.6
  2.2 1.0 %copy-done.6 = bf16[1024,128]{1,0:T(8,128)(2,1)S(1)} copy-done((bf16[1024,128]{1,0:T(8,128)(2,1)S(1)}, bf16[1024,128]{1,0:T(8,128)(2,1)}, u32[]{:S(2)}) %copy-start.6) | copy-done | bytes 262168
  3.2 0.0 copy-start.7
  3.2 0.9 %copy-done.7 = bf16[64,128,3,3]{1,0,3,2:T(8,128)(2,1)S(1)} copy-done((bf16[64,128,3,3]{1,0,3,2:T(8,128)(2,1)S(1)}, bf16[64,128,3,3]{1,0,3,2:T(8,128)(2,1)}, u32[]{:S(2)}) %copy-start.7) | copy-done | bytes 147480
  4.2 0.0 copy-start.8
  4.2 0.7 %copy-done.8 = s32[2,4]{1,0:T(2,128)S(1)} copy-done((s32[2,4]{1,0:T(2,128)S(1)}, s32[2,4]{1,0:T(2,128)}, u32[]{:S(2)}) %copy-start.8) | copy-done | bytes 56
  4.8 0.0 copy-start.4
  4.8 0.0 copy-start.9
  4.8 0.0 copy-start.10
  4.8 0.0 copy-start.11
  4.8 12.0 %exchange.1 = (bf16[4,128,1024]{2,1,0:T(8,128)(2,1)S(1)}, bf16[256,1024]{1,0:T(8,128)(2,1)S(1)}, bf16[2,9,64,128]{3,2,1,0:T(8,128)(2,1)S(1)}, bf16[2,128,128]{2,1,0:T(8,128)(2,1)S(1)}, bf16[3,128,128]{2,1,0:T(8,128)(2,1)S(1)}) custom-call(s32[2,4]{1,0:T(2,128)S(1)} %copy-done.8, bf16[8,64,1024]{2,1,0:T(8,128)(2,1)S(1)} %copy-done.1, ...), custom_call_target="tpu_custom_call" | custom-call | tf_op jit(solution)/shard_map/exchange/pallas_call | solution.py:424
  16.8 0.0 copy-done.2
  16.8 0.0 copy-done.4
  16.8 0.0 copy-done.9
  16.8 0.0 copy-done.10
  16.9 0.0 copy-done.11
  16.9 0.0 copy-start.5
  16.9 1.0 %copy-done.5 = bf16[512,512]{1,0:T(8,128)(2,1)S(1)} copy-done((bf16[512,512]{1,0:T(8,128)(2,1)S(1)}, bf16[512,512]{1,0:T(8,128)(2,1)}, u32[]{:S(2)}) %copy-start.5) | copy-done | bytes 524312
  17.9 7.6 %group_step.1 = (bf16[2,128,1024]{2,1,0:T(8,128)(2,1)S(1)}, f32[32,80,128]{2,1,0:T(8,128)}) custom-call(s32[2,8]{1,0:T(2,128)S(1)} %copy-done.10, s32[2,4]{1,0:T(2,128)S(1)} %copy-done.9, s32[8]{0:T(128)S(1)} %copy-done.11, bf16[4,128,1024]{2,1,0:T(8,128)(2,1)S(1)} %get-tuple-element.13.full, bf16[256,1024]{1,0:T(8,128)(2,1)S(1)} %get-tuple-element.14.grad, ...), custom_call_target="tpu_custom_call" | custom-call | tf_op jit(solution)/shard_map/group_step/pallas_call | solution.py:569
  25.5 0.0 copy-start
  25.5 1.3 %copy-done = f32[32,80,128]{2,1,0:T(8,128)S(1)} copy-done((f32[32,80,128]{2,1,0:T(8,128)S(1)}, f32[32,80,128]{2,1,0:T(8,128)}, u32[]{:S(2)}) %copy-start) | copy-done | bytes 1310744
  26.8 22.8 %finish.1 = (f32[1152,128]{1,0:T(8,128)S(1)}, f32[512,256]{1,0:T(8,128)S(1)}, bf16[2,128,1024]{2,1,0:T(8,128)(2,1)S(1)}) custom-call(f32[2,16,80,128]{3,2,1,0:T(8,128)S(1)} %bitcast.25, bf16[2,128,1024]{2,1,0:T(8,128)(2,1)S(1)} %get-tuple-element.19.refs_1_), custom_call_target="tpu_custom_call" | custom-call | tf_op jit(solution)/shard_map/finish/pallas_call | solution.py:664
  49.6 1.1 %copy.22 = f32[4,128,256]{2,0,1:T(4,128)} copy(f32[4,128,256]{2,1,0:T(8,128)S(1)} %bitcast.27) | data formatting | bytes 1048576 | tf_op jit(solution)/shard_map/reshape | solution.py:703
  50.8 0.8 %copy.26 = bf16[2,128,1024]{2,1,0:T(8,128)(2,1)} copy(bf16[2,128,1024]{2,1,0:T(8,128)(2,1)S(1)} %get-tuple-element.28) | data formatting | bytes 1048576
  51.5 0.8 %copy.27 = f32[128,128,3,3]{1,0,3,2:T(8,128)} copy(f32[128,128,3,3]{1,0,3,2:T(8,128)S(1)} %bitcast.26) | data formatting | bytes 1179648
  (1 shorter events, 0.0 us)
Async XLA Ops:
  0.6 1.6 %copy-start.3 = (bf16[2,128,1024]{2,1,0:T(8,128)(2,1)S(1)}, bf16[2,128,1024]{2,1,0:T(8,128)(2,1)}, u32[]{:S(2)}) copy-start(bf16[2,128,1024]{2,1,0:T(8,128)(2,1)} %refs_2_.1) | copy-start | bytes 1572868
  0.6 1.6 %copy-start.1 = (bf16[8,64,1024]{2,1,0:T(8,128)(2,1)S(1)}, bf16[8,64,1024]{2,1,0:T(8,128)(2,1)}, u32[]{:S(2)}) copy-start(bf16[8,64,1024]{2,1,0:T(8,128)(2,1)} %refs_1_.1) | copy-start | bytes 3145732
  2.0 14.8 %copy-start.2 = (bf16[2,512,512]{2,1,0:T(8,128)(2,1)S(1)}, bf16[2,512,512]{2,1,0:T(8,128)(2,1)}, u32[]{:S(2)}) copy-start(bf16[2,512,512]{2,1,0:T(8,128)(2,1)} %constant.11.clone.rows) | copy-start | bytes 3145732
  2.2 1.0 %copy-start.6 = (bf16[1024,128]{1,0:T(8,128)(2,1)S(1)}, bf16[1024,128]{1,0:T(8,128)(2,1)}, u32[]{:S(2)}) copy-start(bf16[1024,128]{1,0:T(8,128)(2,1)} %constant.8.clone.refs_4_) | copy-start | bytes 786436
  3.2 0.9 %copy-start.7 = (bf16[64,128,3,3]{1,0,3,2:T(8,128)(2,1)S(1)}, bf16[64,128,3,3]{1,0,3,2:T(8,128)(2,1)}, u32[]{:S(2)}) copy-start(bf16[64,128,3,3]{1,0,3,2:T(8,128)(2,1)} %param.12) | copy-start | bytes 442372
  4.2 0.7 %copy-start.8 = (s32[2,4]{1,0:T(2,128)S(1)}, s32[2,4]{1,0:T(2,128)}, u32[]{:S(2)}) copy-start(s32[2,4]{1,0:T(2,128)} %ids.1) | copy-start | bytes 100
  4.8 12.0 %copy-start.4 = (bf16[256,1024]{1,0:T(8,128)(2,1)S(1)}, bf16[256,1024]{1,0:T(8,128)(2,1)}, u32[]{:S(2)}) copy-start(bf16[256,1024]{1,0:T(8,128)(2,1)} %constant.10.clone.columns) | copy-start | bytes 1572868
  4.8 12.0 %copy-start.9 = (s32[2,4]{1,0:T(2,128)S(1)}, s32[2,4]{1,0:T(2,128)}, u32[]{:S(2)}) copy-start(s32[2,4]{1,0:T(2,128)} %ids.1) | copy-start | bytes 100
  4.8 12.0 %copy-start.10 = (s32[2,8]{1,0:T(2,128)S(1)}, s32[2,8]{1,0:T(2,128)}, u32[]{:S(2)}) copy-start(s32[2,8]{1,0:T(2,128)} %near_groups.1) | copy-start | bytes 196
  4.8 12.0 %copy-start.11 = (s32[8]{0:T(128)S(1)}, s32[8]{0:T(128)}, u32[]{:S(2)}) copy-start(s32[8]{0:T(128)} %tissue.1) | copy-start | bytes 100
  16.9 1.0 %copy-start.5 = (bf16[512,512]{1,0:T(8,128)(2,1)S(1)}, bf16[512,512]{1,0:T(8,128)(2,1)}, u32[]{:S(2)}) copy-start(bf16[512,512]{1,0:T(8,128)(2,1)} %constant.9.clone.phases) | copy-start | bytes 1572868
  25.5 1.3 %copy-start = (f32[32,80,128]{2,1,0:T(8,128)S(1)}, f32[32,80,128]{2,1,0:T(8,128)}, u32[]{:S(2)}) copy-start(f32[32,80,128]{2,1,0:T(8,128)} %get-tuple-element.18) | copy-start | bytes 3932164

commit v4 on v3

--- a/solution.py
+++ b/solution.py
@@ -589,13 +589,22 @@
 
 
 def finish_kernel(
-    n, part_ref, mine_ref, conv_ref, mix_ref, merged_ref, out_ref, near, held, recv,
-    send_a, recv_a, send_b, recv_b, send_c, recv_c, chip_send, chip_recv,
+    part_ref, mine_ref, conv_ref, mix_ref, merged_ref, out_ref, near, held, flat, mid, middle,
+    tall, send_a, recv_a, send_b, recv_b, send_c, recv_c, send_d, recv_d, send_e, recv_e,
+    chip_send, chip_recv,
 ):
     me = lax.axis_index("tile")
     core = lax.axis_index("chan")
+    z = me // 4
+    q = lax.rem(me, 4)
     other = 1 - core
     barrier = pltpu.get_barrier_semaphore()
+
+    def beside(d):
+        return lax.rem(q + d, 4)
+
+    def above(d):
+        return lax.rem(z + d, 4)
 
     def remote(src, dst, send_sem, recv_sem, row, column):
         copy = pltpu.make_async_remote_copy(
@@ -609,13 +618,12 @@
         copy.start()
         return copy
 
-    for d in range(1, n):
-        pl.semaphore_signal(
-            barrier, inc=1, device_id=(lax.rem(me + d, n), core), device_id_type=MESH
-        )
     pl.semaphore_signal(barrier, inc=1, device_id=(me, other), device_id_type=MESH)
+    for d in range(1, 4):
+        for row in (4 * z + beside(d), 4 * above(d) + q):
+            pl.semaphore_signal(barrier, inc=1, device_id=(row, core), device_id_type=MESH)
     held[...] = part_ref[other].astype(held.dtype)
-    pl.semaphore_wait(barrier, n)
+    pl.semaphore_wait(barrier, 7)
 
     over = remote(held, near, chip_send.at[0], chip_recv.at[0], me, other)
     swap = remote(
@@ -625,44 +633,69 @@
     over.wait()
     held[...] = (part_ref[core] + near[...].astype(jnp.float32)).astype(held.dtype)
 
-    scatter = []
-    for d in range(1, n):
-        peer = lax.rem(me + d, n)
-        scatter.append(remote(held.at[peer], recv.at[d], send_a.at[d], recv_a.at[d], peer, core))
-    total = part_ref[core, me] + near[me].astype(jnp.float32)
-    for d in range(1, n):
-        scatter[d - 1].wait_recv()
-        total += recv[d].astype(jnp.float32)
-    out_ref[core, me] = total.astype(out_ref.dtype)
-
+    sent = []
+    across = []
+    for d in range(1, 4):
+        across.append(
+            remote(
+                held.at[:, beside(d)], flat.at[d], send_a.at[d], recv_a.at[d],
+                4 * z + beside(d), core,
+            )
+        )
+    total = part_ref[core, :, q] + near[:, q].astype(jnp.float32)
+    for d in range(1, 4):
+        across[d - 1].wait_recv()
+        total += flat[d].astype(jnp.float32)
+    middle[...] = total
+    mid[...] = total.astype(mid.dtype)
+    along = []
+    for d in range(1, 4):
+        along.append(
+            remote(
+                mid.at[above(d)], tall.at[d], send_b.at[d], recv_b.at[d], 4 * above(d) + q, core
+            )
+        )
+    last = middle[z]
+    for d in range(1, 4):
+        along[d - 1].wait_recv()
+        last += tall[d].astype(jnp.float32)
+    out_ref[core, z, q] = last.astype(out_ref.dtype)
+
+    own = out_ref.at[core, z, q]
+    column = out_ref.at[core, :, q]
+    raised = []
+    for d in range(1, 4):
+        raised.append(remote(own, own, send_c.at[d], recv_c.at[d], 4 * above(d) + q, core))
+    for copy in raised:
+        copy.wait_recv()
     spread = []
-    for d in range(1, n):
-        own = out_ref.at[core, me]
-        spread.append(remote(own, own, send_b.at[d], recv_b.at[d], lax.rem(me + d, n), core))
-    own = out_ref.at[core, me]
-    crossing = [remote(own, own, send_c.at[0], recv_c.at[0], me, other)]
-    for d in range(1, n):
+    for d in range(1, 4):
+        spread.append(
+            remote(column, column, send_d.at[d], recv_d.at[d], 4 * z + beside(d), core)
+        )
+    crossing = [remote(column, column, send_e.at[0], recv_e.at[0], me, other)]
+    for d in range(1, 4):
         spread[d - 1].wait_recv()
-        piece = out_ref.at[core, lax.rem(me + n - d, n)]
-        crossing.append(remote(piece, piece, send_c.at[d], recv_c.at[d], me, other))
-    for copy in scatter + spread:
+        column = out_ref.at[core, :, lax.rem(q + 4 - d, 4)]
+        crossing.append(remote(column, column, send_e.at[d], recv_e.at[d], me, other))
+    for copy in across + along + raised + spread:
         copy.wait_send()
     swap.wait()
     for copy in crossing:
         copy.wait()
     for piece in range(32):
-        block = out_ref[piece // n, piece % n].astype(jnp.float32)
+        block = out_ref[piece // 16, (piece % 16) // 4, piece % 4].astype(jnp.float32)
         conv_ref[pl.ds(36 * piece, 36), :] = block[:36]
         mix_ref[pl.ds(16 * piece, 16), :128] = block[48:64]
         mix_ref[pl.ds(16 * piece, 16), 128:] = block[64:]
 
 
-def finish(parts, mine, n):
+def finish(parts, mine):
     bf = jnp.bfloat16
-    rows = parts.shape[2]
+    rows = parts.shape[3]
     vmem = pl.BlockSpec(memory_space=pltpu.VMEM)
     return pl.pallas_call(
-        lambda *refs: finish_kernel(n, *refs),
+        finish_kernel,
         name="finish",
         out_shape=(
             jax.ShapeDtypeStruct((1152, LANES), jnp.float32),
@@ -671,9 +704,14 @@
         ),
         in_specs=[vmem] * 2,
         out_specs=(vmem, vmem, vmem),
-        scratch_shapes=[pltpu.VMEM((2, n, rows, LANES), bf)]
-        + [pltpu.VMEM((n, rows, LANES), bf)] * 3
-        + [pltpu.SemaphoreType.DMA((n,))] * 6
+        scratch_shapes=[pltpu.VMEM((2, 4, 4, rows, LANES), bf)]
+        + [pltpu.VMEM((4, 4, rows, LANES), bf)] * 3
+        + [
+            pltpu.VMEM((4, rows, LANES), bf),
+            pltpu.VMEM((4, rows, LANES), jnp.float32),
+            pltpu.VMEM((4, rows, LANES), bf),
+        ]
+        + [pltpu.SemaphoreType.DMA((4,))] * 10
         + [pltpu.SemaphoreType.DMA((2,))] * 2,
         compiler_params=pltpu.CompilerParams(
             collective_id=2, has_side_effects=True, vmem_limit_bytes=32 << 20
@@ -698,7 +736,7 @@
         neighbours, group_tiles, tissue, full, grad_full, weight_full, side, cap, mix, mix.T,
         jnp.asarray(phase_picker()), jnp.asarray(column_picker()), jnp.asarray(row_picker()),
     )
-    summed_conv, summed_mix, merged = finish(parts.reshape(2, n, 80, LANES), merged_all, n)
+    summed_conv, summed_mix, merged = finish(parts.reshape(2, 4, 4, 80, LANES), merged_all)
     grad_conv = summed_conv.reshape(3, 3, 128, 128).transpose(2, 3, 0, 1)
     grad_merge = summed_mix.reshape(4, 128, 256).transpose(1, 0, 2)
     return merged, grad_conv, grad_merge

time: 53 us -> 53.8 us (1.015)
  Pallas kernels: 42.3 us -> 43.5 us
    pallas_call x1, Pallas kernels: 22.8 us -> 24 us  [finish(): pl.pallas_call(finish_kernel, name='finish', out_shape=(jax.ShapeDtypeStr...]
where the time goes in v4:
time: 53.8 us; the launch traced here: 53.6 us
  Pallas kernels  43.5 us (81%)
  local copies, waits for them, and re-layouts  9.24 us (17%)
  between operations  0.77 us (1%)
    pallas_call x1, Pallas kernels, finish(): pl.pallas_call(finish_kernel, name='finish', out_shape=(jax.ShapeDtypeStr...  24 us
    pallas_call x1, Pallas kernels, exchange(): pl.pallas_call(lambda *refs: exchange_kernel(n, *refs), name='exchange',...  12 us
    pallas_call x1, Pallas kernels, group_step(): pl.pallas_call(group_kernel, name='group_step', out_shape=(jax.ShapeDtype...  7.58 us
    unnamed x27, local copies, waits for them, and re-layouts  6.66 us
    transpose x1, local copies, waits for them, and re-layouts, group_per_core(): mix = merge_weight.transpose(1, 0, 2).reshape(512, 256)  1.32 us
    reshape x1, local copies, waits for them, and re-layouts, group_per_core(): grad_merge = summed_mix.reshape(4, 128, 256).transpose(1, 0, 2)  1.13 us

profile of v4, /device:TPU:0, one launch (start us, length us, event | category | flops | bytes accessed | tf_op | source)
XLA Modules:
  0.0 53.6 jit_solution(215856011801320895)
XLA Ops:
  0.6 0.0 copy-start.3
  0.6 0.0 copy-start.1
  0.7 1.3 %copy.14 = bf16[4,128,256]{1,0,2:T(4,128)(2,1)S(1)} copy(bf16[4,128,256]{2,0,1:T(4,128)(2,1)} %bitcast.31) | data formatting | bytes 524288 | tf_op jit(solution)/shard_map/transpose | solution.py:734
  2.0 0.0 copy-start.2
  2.0 0.1 copy.15.mix
  2.2 0.0 copy-done.3
  2.2 0.0 copy-done.1
  2.2 0.0 copy-start.6
  2.2 1.0 %copy-done.6 = bf16[1024,128]{1,0:T(8,128)(2,1)S(1)} copy-done((bf16[1024,128]{1,0:T(8,128)(2,1)S(1)}, bf16[1024,128]{1,0:T(8,128)(2,1)}, u32[]{:S(2)}) %copy-start.6) | copy-done | bytes 262168
  3.2 0.0 copy-start.7
  3.2 0.9 %copy-done.7 = bf16[64,128,3,3]{1,0,3,2:T(8,128)(2,1)S(1)} copy-done((bf16[64,128,3,3]{1,0,3,2:T(8,128)(2,1)S(1)}, bf16[64,128,3,3]{1,0,3,2:T(8,128)(2,1)}, u32[]{:S(2)}) %copy-start.7) | copy-done | bytes 147480
  4.2 0.0 copy-start.8
  4.2 0.7 %copy-done.8 = s32[2,4]{1,0:T(2,128)S(1)} copy-done((s32[2,4]{1,0:T(2,128)S(1)}, s32[2,4]{1,0:T(2,128)}, u32[]{:S(2)}) %copy-start.8) | copy-done | bytes 56
  4.8 0.0 copy-start.4
  4.8 0.0 copy-start.9
  4.8 0.0 copy-start.10
  4.8 0.0 copy-start.11
  4.8 12.0 %exchange.1 = (bf16[4,128,1024]{2,1,0:T(8,128)(2,1)S(1)}, bf16[256,1024]{1,0:T(8,128)(2,1)S(1)}, bf16[2,9,64,128]{3,2,1,0:T(8,128)(2,1)S(1)}, bf16[2,128,128]{2,1,0:T(8,128)(2,1)S(1)}, bf16[3,128,128]{2,1,0:T(8,128)(2,1)S(1)}) custom-call(s32[2,4]{1,0:T(2,128)S(1)} %copy-done.8, bf16[8,64,1024]{2,1,0:T(8,128)(2,1)S(1)} %copy-done.1, ...), custom_call_target="tpu_custom_call" | custom-call | tf_op jit(solution)/shard_map/exchange/pallas_call | solution.py:424
  16.8 0.0 copy-done.2
  16.8 0.0 copy-done.4
  16.8 0.0 copy-done.9
  16.8 0.0 copy-done.10
  16.9 0.0 copy-done.11
  16.9 0.0 copy-start.5
  16.9 1.0 %copy-done.5 = bf16[512,512]{1,0:T(8,128)(2,1)S(1)} copy-done((bf16[512,512]{1,0:T(8,128)(2,1)S(1)}, bf16[512,512]{1,0:T(8,128)(2,1)}, u32[]{:S(2)}) %copy-start.5) | copy-done | bytes 524312
  17.9 7.6 %group_step.1 = (bf16[2,128,1024]{2,1,0:T(8,128)(2,1)S(1)}, f32[32,80,128]{2,1,0:T(8,128)}) custom-call(s32[2,8]{1,0:T(2,128)S(1)} %copy-done.10, s32[2,4]{1,0:T(2,128)S(1)} %copy-done.9, s32[8]{0:T(128)S(1)} %copy-done.11, bf16[4,128,1024]{2,1,0:T(8,128)(2,1)S(1)} %get-tuple-element.13.full, bf16[256,1024]{1,0:T(8,128)(2,1)S(1)} %get-tuple-element.14.grad, ...), custom_call_target="tpu_custom_call" | custom-call | tf_op jit(solution)/shard_map/group_step/pallas_call | solution.py:569
  25.5 0.0 copy-start
  25.5 1.3 %copy-done = f32[32,80,128]{2,1,0:T(8,128)S(1)} copy-done((f32[32,80,128]{2,1,0:T(8,128)S(1)}, f32[32,80,128]{2,1,0:T(8,128)}, u32[]{:S(2)}) %copy-start) | copy-done | bytes 1310744
  26.8 24.0 %finish.1 = (f32[1152,128]{1,0:T(8,128)S(1)}, f32[512,256]{1,0:T(8,128)S(1)}, bf16[2,128,1024]{2,1,0:T(8,128)(2,1)S(1)}) custom-call(f32[2,4,4,80,128]{4,3,2,1,0:T(8,128)S(1)} %bitcast.25, bf16[2,128,1024]{2,1,0:T(8,128)(2,1)S(1)} %get-tuple-element.19.mine_ref), custom_call_target="tpu_custom_call" | custom-call | tf_op jit(solution)/shard_map/finish/pallas_call | solution.py:697
  50.8 1.1 %copy.22 = f32[4,128,256]{2,0,1:T(4,128)} copy(f32[4,128,256]{2,1,0:T(8,128)S(1)} %bitcast.27) | data formatting | bytes 1048576 | tf_op jit(solution)/shard_map/reshape | solution.py:741
  51.9 0.8 %copy.26 = bf16[2,128,1024]{2,1,0:T(8,128)(2,1)} copy(bf16[2,128,1024]{2,1,0:T(8,128)(2,1)S(1)} %get-tuple-element.28) | data formatting | bytes 1048576
  52.7 0.8 %copy.27 = f32[128,128,3,3]{1,0,3,2:T(8,128)} copy(f32[128,128,3,3]{1,0,3,2:T(8,128)S(1)} %bitcast.26) | data formatting | bytes 1179648
  (1 shorter events, 0.0 us)
Async XLA Ops:
  0.6 1.6 %copy-start.3 = (bf16[2,128,1024]{2,1,0:T(8,128)(2,1)S(1)}, bf16[2,128,1024]{2,1,0:T(8,128)(2,1)}, u32[]{:S(2)}) copy-start(bf16[2,128,1024]{2,1,0:T(8,128)(2,1)} %refs_2_.1) | copy-start | bytes 1572868
  0.6 1.6 %copy-start.1 = (bf16[8,64,1024]{2,1,0:T(8,128)(2,1)S(1)}, bf16[8,64,1024]{2,1,0:T(8,128)(2,1)}, u32[]{:S(2)}) copy-start(bf16[8,64,1024]{2,1,0:T(8,128)(2,1)} %refs_1_.1) | copy-start | bytes 3145732
  2.0 14.8 %copy-start.2 = (bf16[2,512,512]{2,1,0:T(8,128)(2,1)S(1)}, bf16[2,512,512]{2,1,0:T(8,128)(2,1)}, u32[]{:S(2)}) copy-start(bf16[2,512,512]{2,1,0:T(8,128)(2,1)} %constant.11.clone.rows) | copy-start | bytes 3145732
  2.2 1.0 %copy-start.6 = (bf16[1024,128]{1,0:T(8,128)(2,1)S(1)}, bf16[1024,128]{1,0:T(8,128)(2,1)}, u32[]{:S(2)}) copy-start(bf16[1024,128]{1,0:T(8,128)(2,1)} %constant.8.clone.refs_4_) | copy-start | bytes 786436
  3.2 0.9 %copy-start.7 = (bf16[64,128,3,3]{1,0,3,2:T(8,128)(2,1)S(1)}, bf16[64,128,3,3]{1,0,3,2:T(8,128)(2,1)}, u32[]{:S(2)}) copy-start(bf16[64,128,3,3]{1,0,3,2:T(8,128)(2,1)} %param.12) | copy-start | bytes 442372
  4.2 0.7 %copy-start.8 = (s32[2,4]{1,0:T(2,128)S(1)}, s32[2,4]{1,0:T(2,128)}, u32[]{:S(2)}) copy-start(s32[2,4]{1,0:T(2,128)} %ids.1) | copy-start | bytes 100
  4.8 12.0 %copy-start.4 = (bf16[256,1024]{1,0:T(8,128)(2,1)S(1)}, bf16[256,1024]{1,0:T(8,128)(2,1)}, u32[]{:S(2)}) copy-start(bf16[256,1024]{1,0:T(8,128)(2,1)} %constant.10.clone.columns) | copy-start | bytes 1572868
  4.8 12.0 %copy-start.9 = (s32[2,4]{1,0:T(2,128)S(1)}, s32[2,4]{1,0:T(2,128)}, u32[]{:S(2)}) copy-start(s32[2,4]{1,0:T(2,128)} %ids.1) | copy-start | bytes 100
  4.8 12.0 %copy-start.10 = (s32[2,8]{1,0:T(2,128)S(1)}, s32[2,8]{1,0:T(2,128)}, u32[]{:S(2)}) copy-start(s32[2,8]{1,0:T(2,128)} %near_groups.1) | copy-start | bytes 196
  4.8 12.0 %copy-start.11 = (s32[8]{0:T(128)S(1)}, s32[8]{0:T(128)}, u32[]{:S(2)}) copy-start(s32[8]{0:T(128)} %tissue.1) | copy-start | bytes 100
  16.9 1.0 %copy-start.5 = (bf16[512,512]{1,0:T(8,128)(2,1)S(1)}, bf16[512,512]{1,0:T(8,128)(2,1)}, u32[]{:S(2)}) copy-start(bf16[512,512]{1,0:T(8,128)(2,1)} %constant.9.clone.phases) | copy-start | bytes 1572868
  25.5 1.3 %copy-start = (f32[32,80,128]{2,1,0:T(8,128)S(1)}, f32[32,80,128]{2,1,0:T(8,128)}, u32[]{:S(2)}) copy-start(f32[32,80,128]{2,1,0:T(8,128)} %get-tuple-element.18) | copy-start | bytes 3932164
